TPU v7x, 256 devices: a whole 4x4x8 slice. The times are simulated.
256 devices in a mesh: elem: 16 (over y, z_hi), grp: 16 (over z_lo, x, core).
Axes of the slice: x: 4, y: 4, z: 8 (z_hi: 4, z_lo: 2; z = z_hi * 2 + z_lo), core: 2. Of those that a mesh axis runs over, the one named last changes fastest.
Arguments:
- basis_values: bfloat16 [16, 1024, 32768], P('elem', 'grp'), may hold values from -0.03125 to 0.03125
- basis_derivs: bfloat16 [16, 1024, 32768], P('elem', 'grp'), may hold values from -0.03125 to 0.03125
- potential: float32 [16, 32768], P('elem', 'grp'), may hold values from 0.5 to 2
- hop_blocks: bfloat16 [16, 4, 1024, 1024], P('elem', None, 'grp'), may hold values from -0.1875 to 0.1875
- coeffs: bfloat16 [16, 1024, 4096], P('elem', None, 'grp'), may hold values from -6 to 6
- counts: int32 [16], replicated, may hold values from 256 to 1024, as said below
- neighbours: int32 [16, 4], replicated, may hold values from 0 to 15, as said below
Outputs:
- applied_bands: float32 [16, 1024, 4096], P('elem', None, 'grp')
Inputs may be any that keep to these rules, and one draw needn't show every extreme that they name: `counts`: count of live basis functions of each element; some element has exactly 1024 and some exactly 256. `neighbours`: four distinct elements, none the element itself.
All inputs are finite; a program needn't handle non-finite values.
Results may differ from a plain program's by a relative error of at most 0.0022.
Values may be sent and summed in bfloat16 or wider, within the bound.
No kernel may reach another device: no remote copies, remote signals or barrier semaphores. Data moves between devices by JAX's collectives and lax.ppermute only.
A program may use at most 192 MiB of HBM per device.

v0:
```python
import jax
import jax.numpy as jnp
from jax import lax
from jax.sharding import PartitionSpec as P


def local(basis_values, basis_derivs, potential, hop_blocks, coeffs, counts, neighbours):
    values_slab, derivs_slab = (
        lax.all_to_all(basis_values, "grp", split_axis=2, concat_axis=1, tiled=True),
        lax.all_to_all(basis_derivs, "grp", split_axis=2, concat_axis=1, tiled=True),
    )
    values_slab = values_slab[0]
    derivs_slab = derivs_slab[0]
    weighted = (potential[0][None, :] * values_slab.astype(jnp.float32)).astype(jnp.bfloat16)
    partial_value = 0.5 * jnp.einsum(
        "ip,jp->ij", derivs_slab, derivs_slab, preferred_element_type=jnp.float32
    )
    partial_value = partial_value + jnp.einsum(
        "ip,jp->ij", values_slab, weighted, preferred_element_type=jnp.float32
    )
    element = lax.axis_index("elem")
    width = coeffs.shape[1]
    row_ids = jnp.arange(width, dtype=jnp.int32)
    live_rows = row_ids < counts[element]
    own_coeffs = jnp.where(live_rows[:, None], coeffs[0], jnp.zeros_like(coeffs[0]))
    near_ids = neighbours[element]
    initial = jnp.zeros((near_ids.shape[0], width, coeffs.shape[2]), jnp.bfloat16)
    pieces = lax.all_gather(own_coeffs[None], "elem", axis=0, tiled=True)
    inside = (near_ids >= 0) & (near_ids < pieces.shape[0])
    clipped = jnp.clip(near_ids, 0, pieces.shape[0] - 1)
    picked = jnp.take(pieces, clipped, axis=0)
    near_coeffs = jnp.where(inside[:, None, None], picked, initial)
    assembled_low = lax.psum(partial_value, "grp").astype(jnp.bfloat16)
    applied = jnp.dot(assembled_low, own_coeffs, preferred_element_type=jnp.float32)
    applied = applied + jnp.einsum(
        "krm,kmb->rb",
        lax.all_gather(hop_blocks, "grp", axis=2, tiled=True)[0],
        near_coeffs,
        preferred_element_type=jnp.float32,
    )
    result = jnp.where(live_rows[:, None], applied, jnp.zeros_like(applied))
    return result[None]


def solution(mesh):
    placed = (
        P("elem", "grp", None),
        P("elem", "grp", None),
        P("elem", "grp"),
        P("elem", None, "grp", None),
        P("elem", None, "grp"),
        P(),
        P(),
    )
    return jax.shard_map(
        local, mesh=mesh, in_specs=placed, out_specs=P("elem", None, "grp"), check_vma=False
    )
```

profile of v0, /device:TPU:80, one launch (start us, length us, event | category | flops | bytes accessed | tf_op | source)
XLA Modules:
  0.0 701.6 jit_solution(7033604246611813933)
XLA Ops:
  6.5 1.2 dynamic_slice.6
  7.8 0.6 iota_compare_fusion
  8.4 2.0 broadcast_select_fusion
  10.5 33.2 %copy.18 = bf16[1,64,32768]{1,0,2:T(2,128)(2,1)} copy(bf16[1,64,32768]{2,1,0:T(8,128)(2,1)} %param.8) | data formatting | bytes 8388608 | tf_op args[1]
  43.7 0.5 broadcast.115
  44.2 179.1 %reduce.5 = bf16[32768,64]{1,0:T(8,128)(2,1)} reduce(bf16[32768,1,64]{2,1,0:T(2,128)(2,1)} %bitcast.57, bf16[]{:T(256)} %broadcast.115), dimensions={1}, to_apply=%bitcast.43.reduce_sub_computation | reduce | bytes 8388610
  223.3 14.0 %reshape.77 = bf16[16,2,65536]{2,1,0:T(2,128)(2,1)} reshape(bf16[32768,64]{1,0:T(8,128)(2,1)} %reduce.5) | data formatting | bytes 8388608
  237.2 5.8 all-to-all-start
  243.1 0.3 all-gather.5.cloned.1.call-start
  243.4 0.4 all-gather.5.cloned.1.call-update
  243.8 33.2 %copy.21 = bf16[1,64,32768]{1,0,2:T(2,128)(2,1)} copy(bf16[1,64,32768]{2,1,0:T(8,128)(2,1)} %param.7) | data formatting | bytes 8388608 | tf_op args[0]
  277.0 179.1 %reduce.6 = bf16[32768,64]{1,0:T(8,128)(2,1)} reduce(bf16[32768,1,64]{2,1,0:T(2,128)(2,1)} %bitcast.58, bf16[]{:T(256)} %broadcast.115), dimensions={1}, to_apply=%bitcast.45.reduce_sub_computation | reduce | bytes 8388610
  456.1 14.0 %reshape.79 = bf16[16,2,65536]{2,1,0:T(2,128)(2,1)} reshape(bf16[32768,64]{1,0:T(8,128)(2,1)} %reduce.6) | data formatting | bytes 8388608
  470.0 6.4 all-to-all-start.1
  476.8 14.7 %reshape.78 = bf16[32768,1,64]{2,1,0:T(2,128)(2,1)} reshape(bf16[16,2,65536]{2,1,0:T(2,128)(2,1)} %all-to-all-done) | data formatting | bytes 8388608
  491.5 32.1 %copy.19 = bf16[1,64,32768]{2,1,0:T(8,128)(2,1)} copy(bf16[1,64,32768]{1,0,2:T(2,128)(2,1)} %bitcast.55) | data formatting | bytes 8388608 | tf_op jit(solution)/shard_map/all_to_all | solution.py:10
  523.6 4.6 copy.32
  528.2 0.6 bitcast_bitcast_fusion.1
  528.8 4.3 copy.20
  533.1 14.7 %reshape.80 = bf16[32768,1,64]{2,1,0:T(2,128)(2,1)} reshape(bf16[16,2,65536]{2,1,0:T(2,128)(2,1)} %all-to-all-done.1) | data formatting | bytes 8388608
  547.8 32.2 %copy.22 = bf16[1,64,32768]{2,1,0:T(8,128)(2,1)} copy(bf16[1,64,32768]{1,0,2:T(2,128)(2,1)} %bitcast.56) | data formatting | bytes 8388608 | tf_op jit(solution)/shard_map/all_to_all | solution.py:9
  580.1 4.6 copy.33
  584.7 1.4 multiply_convert_fusion
  586.0 2.3 copy.23
  588.3 0.6 bitcast_bitcast_fusion
  588.9 2.3 copy.24
  591.2 4.8 fusion.30
  596.0 6.1 bitcast_add_fusion
  602.1 78.7 %all-reduce.1 = bf16[1024,1024]{1,0:T(8,128)(2,1)S(1)} all-reduce(f32[1024,1024]{1,0:T(8,128)} %bitcast_add_fusion), channel_id=1, replica_groups=mesh['elem'=16,'grp'=16] {'grp'}, use_global_device_ids=true, to_apply=%region_0.1 | all-reduce | flops 1048576 | bytes 6291456 | tf_op jit(solution)/shard_map/psum | solution.py:33
  680.9 5.4 gather_fusion
  686.3 6.4 fusion.17
  692.8 1.8 fusion.14
  (19 shorter events, 0.5 us)
Async XLA Ops:
  6.5 674.3 %all-gather.3.cloned.1.call-start = ((), (), s32[]{:S(2)}) async-start(), calls=%async_computation.2 | async-start | bytes 8912896 | tf_op jit(solution)/shard_map/all_gather | solution.py:28
  237.2 232.8 %all-to-all-start = ((bf16[16,2,65536]{2,1,0:T(2,128)(2,1)}), bf16[16,2,65536]{2,1,0:T(2,128)(2,1)}, u32[]{:S(2)}, u32[]{:S(2)}) async-start(bf16[16,2,65536]{2,1,0:T(2,128)(2,1)} %reshape.77), calls=%async_computation | async-start | bytes 8388608 | tf_op jit(solution)/shard_map/all_to_all | solution.py:10
  243.1 443.2 %all-gather.5.cloned.1.call-start = ((), (), s32[]{:S(2)}) async-start(), calls=%async_computation.3 | async-start | bytes 8912896 | tf_op jit(solution)/shard_map/all_gather | solution.py:37
  470.0 6.4 copy-start.3
  470.0 63.1 %all-to-all-start.1 = ((bf16[16,2,65536]{2,1,0:T(2,128)(2,1)}), bf16[16,2,65536]{2,1,0:T(2,128)(2,1)}, u32[]{:S(2)}, u32[]{:S(2)}) async-start(bf16[16,2,65536]{2,1,0:T(2,128)(2,1)} %reshape.79), calls=%async_computation.1 | async-start | bytes 8388608 | tf_op jit(solution)/shard_map/all_to_all | solution.py:9
  580.0 4.6 copy-start.2
  588.9 2.3 copy-start
  686.3 6.5 copy-start.1
Sparse Core Ops, SparseCore 0:
  10.6 118.3 all-gather.2
  245.7 89.0 all-gather.4
where the time goes:
time: 714 us; the launch traced here: 702 us
  other arithmetic  363 us (51%)
  local copies, waits for them, and re-layouts  214 us (30%)
  blocking collectives  78.7 us (11%)
  matrix products  19.1 us (3%)
  between operations  13.8 us (2%)
  starting transfers between devices  12.6 us (2%)
    unnamed x2, other arithmetic  358 us
    unnamed x17, local copies, waits for them, and re-layouts  133 us
    psum x1, blocking collectives, local(): assembled_low = lax.psum(partial_value, 'grp').astype(jnp.bfloat16)  78.7 us
    all_to_all x3, local copies, waits for them, and re-layouts, local(): lax.all_to_all(basis_derivs, 'grp', split_axis=2, concat_axis=1, tiled=True)  37 us
    all_to_all x3, local copies, waits for them, and re-layouts, local(): lax.all_to_all(basis_values, 'grp', split_axis=2, concat_axis=1, tiled=True)  35.1 us
  transfers between devices with their start and end apart: 4, of which 0 were waited for; matrix products, arithmetic and copies ran while one was open for 83% of the time, Pallas kernels for 0%

commit v1 on v0

v1 whole, which is shorter than its diff:
```python
import jax
import jax.numpy as jnp
from jax import lax
from jax.experimental import pallas as pl
from jax.experimental.pallas import tpu as pltpu
from jax.sharding import Mesh, PartitionSpec as P

ELEM = ("y", "zh")
CHIPS = ("zl", "x")
GRP = ("zl", "x", "c")
CORES = 2


def swap_cores(a):
    return lax.ppermute(a, "c", [(0, 1), (1, 0)])


def spread(a):
    chips = lax.axis_size(CHIPS)
    return lax.all_to_all(
        jnp.broadcast_to(a[None], (chips, *a.shape)), CHIPS, 0, 0, tiled=True
    )


def slab(a):
    rows, points = a.shape
    devices = lax.axis_size(GRP)
    a = a.reshape(rows, devices, points // devices).transpose(1, 0, 2)
    a = lax.all_to_all(a, GRP, 0, 0, tiled=True)
    return a.reshape(devices * rows, points // devices)


def masked_copy(dst, src, count):
    rows = lax.broadcasted_iota(jnp.int32, src.shape, 0)
    src = src.astype(jnp.float32)
    dst[...] = jnp.where(rows < count, src, jnp.zeros_like(src)).astype(dst.dtype)


def hop_kernel(pos, counts, near, mine_ref, other_ref, *refs):
    x_refs, o_ref, masked = refs[:-2], refs[-2], refs[-1]
    step, k = pl.program_id(0), pl.program_id(1)
    width = masked.shape[1]

    @pl.when(step == 0)
    def _():
        for i, x_ref in enumerate(x_refs):

            @pl.when(k == i)
            def _():
                masked_copy(masked.at[i], x_ref[0], counts[near[pos[1], i]])

    def add(a_ref):
        lhs = a_ref[:, 0].reshape(-1, width)
        part = jnp.dot(lhs, masked[k], preferred_element_type=jnp.float32)
        part = part.reshape(o_ref.shape)

        @pl.when(k == 0)
        def _():
            o_ref[...] = part

        @pl.when(k > 0)
        def _():
            o_ref[...] += part

    @pl.when(step == 0)
    def _():
        add(mine_ref)

    @pl.when(step == 1)
    def _():
        add(other_ref)


def hop_apply(pos, counts, near, mine, other, pieces):
    chips, hops, rows, width = mine.shape
    bands = pieces.shape[2]
    picks = [
        pl.BlockSpec(
            (1, width, bands), lambda s, k, pos, cnt, near, i=i: (near[pos[1], i], 0, 0)
        )
        for i in range(hops)
    ]
    block = (chips, 1, rows, width)
    return pl.pallas_call(
        hop_kernel,
        out_shape=jax.ShapeDtypeStruct((chips, CORES, rows, bands), jnp.float32),
        grid_spec=pltpu.PrefetchScalarGridSpec(
            num_scalar_prefetch=3,
            grid=(CORES, hops),
            in_specs=[
                pl.BlockSpec(block, lambda s, k, *_: (0, jnp.where(s == 0, k, hops - 1), 0, 0)),
                pl.BlockSpec(block, lambda s, k, *_: (0, jnp.where(s == 0, 0, k), 0, 0)),
            ]
            + picks,
            out_specs=pl.BlockSpec(
                (chips, 1, rows, bands), lambda s, k, pos, *_: (0, (pos[0] + s) % CORES, 0, 0)
            ),
            scratch_shapes=[pltpu.VMEM((hops, width, bands), jnp.bfloat16)],
        ),
        compiler_params=pltpu.CompilerParams(vmem_limit_bytes=40 << 20),
        cost_estimate=pl.CostEstimate(
            flops=4 * mine.size * bands,
            bytes_accessed=4 * mine.size + 2 * hops * width * bands,
            transcendentals=0,
        ),
        name="hop_apply",
    )(pos, counts, near, mine, other, *([pieces] * hops))


def own_kernel(pos, counts, mine_ref, other_ref, x_ref, h_ref, o_ref, masked):
    step = pl.program_id(0)
    chips, _, rows, bands = o_ref.shape
    width = masked.shape[0]
    count = counts[pos[1]]

    @pl.when(step == 0)
    def _():
        masked_copy(masked, x_ref[0], count)

    def finish(a_ref):
        lhs = a_ref[...].reshape(-1, width)
        part = jnp.dot(lhs, masked[...], preferred_element_type=jnp.float32)
        total = part.reshape(o_ref.shape) + h_ref[...]
        core = (pos[0] + step) % CORES
        at = lax.broadcasted_iota(jnp.int32, o_ref.shape, 0) * (CORES * rows)
        at = at + core * rows + lax.broadcasted_iota(jnp.int32, o_ref.shape, 2)
        o_ref[...] = jnp.where(at < count, total, jnp.zeros_like(total))

    @pl.when(step == 0)
    def _():
        finish(mine_ref)

    @pl.when(step == 1)
    def _():
        finish(other_ref)


def own_apply(pos, counts, mine, other, coeffs, hopped):
    chips, rows, width = mine.shape
    bands = coeffs.shape[2]

    def out_map(s, pos, counts):
        return (0, (pos[0] + s) % CORES, 0, 0)

    whole = pl.BlockSpec((chips, rows, width), lambda s, *_: (0, 0, 0))
    return pl.pallas_call(
        own_kernel,
        out_shape=jax.ShapeDtypeStruct(hopped.shape, jnp.float32),
        grid_spec=pltpu.PrefetchScalarGridSpec(
            num_scalar_prefetch=2,
            grid=(CORES,),
            in_specs=[
                whole,
                whole,
                pl.BlockSpec((1, width, bands), lambda s, *_: (0, 0, 0)),
                pl.BlockSpec((chips, 1, rows, bands), out_map),
            ],
            out_specs=pl.BlockSpec((chips, 1, rows, bands), out_map),
            scratch_shapes=[pltpu.VMEM((width, bands), jnp.bfloat16)],
        ),
        compiler_params=pltpu.CompilerParams(vmem_limit_bytes=40 << 20),
        cost_estimate=pl.CostEstimate(
            flops=4 * mine.size * bands,
            bytes_accessed=4 * mine.size + 2 * width * bands + 8 * hopped.size,
            transcendentals=0,
        ),
        name="own_apply",
    )(pos, counts, mine, other, coeffs, hopped)


def local(basis_values, basis_derivs, potential, hop_blocks, coeffs, counts, neighbours):
    pos = jnp.stack([lax.axis_index("c"), lax.axis_index(ELEM)]).astype(jnp.int32)
    basis_values, pos = lax.optimization_barrier((basis_values, pos))
    values = slab(basis_values[0])
    derivs = slab(basis_derivs[0])

    pieces = lax.all_gather(coeffs, "zh", axis=0, tiled=True)
    pieces = lax.all_gather(pieces, "y", axis=0, tiled=True)
    hops = lax.all_gather(hop_blocks[0], CHIPS, axis=0, tiled=False)
    hopped = hop_apply(pos, counts, neighbours, hops, swap_cores(hops), pieces)

    weighted = (potential[0][None, :] * values.astype(jnp.float32)).astype(jnp.bfloat16)
    part = jnp.einsum("ip,jp->ij", values, weighted, preferred_element_type=jnp.float32)
    part = part + 0.5 * jnp.einsum(
        "ip,jp->ij", derivs, derivs, preferred_element_type=jnp.float32
    )

    chips = lax.axis_size(CHIPS)
    width = part.shape[0]
    rows = width // (chips * CORES)
    part = part.reshape(chips, CORES, rows, width).transpose(1, 0, 2, 3)
    part = lax.all_to_all(part, "c", 0, 0, tiled=True).sum(0)
    part = lax.all_to_all(part, CHIPS, 0, 0, tiled=True).sum(0)
    low = spread(part.astype(jnp.bfloat16))
    result = own_apply(pos, counts, low, swap_cores(low), coeffs, hopped)
    return result.reshape(1, width, coeffs.shape[2])


def solution(mesh):
    fine = Mesh(mesh.devices.reshape(4, 4, 2, 4, 2), ("y", "zh", "zl", "x", "c"))
    placed = (
        P(ELEM, GRP, None),
        P(ELEM, GRP, None),
        P(ELEM, GRP),
        P(ELEM, None, GRP, None),
        P(ELEM, None, GRP),
        P(),
        P(),
    )
    return jax.shard_map(
        local, mesh=fine, in_specs=placed, out_specs=P(ELEM, None, GRP), check_vma=False
    )
```

time: 714 us -> 309 us (0.43); the launches traced: 702 us -> 306 us
  other arithmetic: 363 us -> 7.91 us
  local copies, waits for them, and re-layouts: 214 us -> 20.4 us
  waiting for transfers between devices: 0.45 us -> 184 us
  blocking collectives: 78.7 us -> 27.6 us
  Pallas kernels: 0 us -> 11.9 us
  starting transfers between devices: 12.6 us -> 23.9 us
    unnamed x2 -> x0, other arithmetic: 358 us -> none
    all_to_all x2 -> x3, waiting for transfers between devices: 0.01 us -> 168 us  [the longest x2 142 us: slab(): a = lax.all_to_all(a, GRP, 0, 0, tiled=True)]
    unnamed x17 -> x13, local copies, waits for them, and re-layouts: 133 us -> 11.5 us
    psum x1 -> x0, blocking collectives: 78.7 us -> none  [local(): assembled_low = lax.psum(partial_value, 'grp').astype(jnp.bfloat16)]
    all_to_all x6 -> x0, local copies, waits for them, and re-layouts: 72.1 us -> none  [the longest x3 37 us: local(): lax.all_to_all(basis_derivs, 'grp', split_axis=2, concat_axis=1, tiled=True)]
    all_to_all x0 -> x2, blocking collectives: none -> 27.6 us  [the longest x1 19.4 us: spread(): lax.all_to_all(jnp.broadcast_to(a[None], (chips, *a.shape)), CHIPS, 0, 0,...]
    all_gather x2 -> x3, waiting for transfers between devices: 0.02 us -> 14 us  [the longest x1 14 us: local(): pieces = lax.all_gather(pieces, 'y', axis=0, tiled=True)]
    pallas_call x0 -> x2, Pallas kernels: none -> 11.9 us  [the longest x1 9.41 us: hop_apply(): pl.pallas_call(hop_kernel, out_shape=jax.ShapeDtypeStruct((chips, CORES,...]
  transfers between devices with their start and end apart: 4 -> 8, of which waited for: 0 -> 4; matrix products, arithmetic and copies ran while one was open for 83% -> 11% of each run, Pallas kernels for 0% -> 3%
where the time goes in v1:
time: 309 us; the launch traced here: 306 us
  waiting for transfers between devices  184 us (60%)
  blocking collectives  27.6 us (9%)
  starting transfers between devices  23.9 us (8%)
  local copies, waits for them, and re-layouts  20.4 us (7%)
  matrix products  17.6 us (6%)
  between operations  13.2 us (4%)
  Pallas kernels  11.9 us (4%)
  other arithmetic  7.91 us (3%)
    all_to_all x2, waiting for transfers between devices, slab(): a = lax.all_to_all(a, GRP, 0, 0, tiled=True)  142 us
    all_to_all x1, waiting for transfers between devices, local(): part = lax.all_to_all(part, CHIPS, 0, 0, tiled=True).sum(0)  26.3 us
    all_to_all x2, starting transfers between devices, slab(): a = lax.all_to_all(a, GRP, 0, 0, tiled=True)  19.7 us
    all_to_all x1, blocking collectives, spread(): lax.all_to_all(jnp.broadcast_to(a[None], (chips, *a.shape)), CHIPS, 0, 0,...  19.4 us
    all_gather x1, waiting for transfers between devices, local(): pieces = lax.all_gather(pieces, 'y', axis=0, tiled=True)  14 us
    unnamed x13, local copies, waits for them, and re-layouts  11.5 us
    pallas_call x1, Pallas kernels, hop_apply(): pl.pallas_call(hop_kernel, out_shape=jax.ShapeDtypeStruct((chips, CORES,...  9.41 us
    dot_general x1, matrix products, local(): jnp.einsum('ip,jp->ij', derivs, derivs, preferred_element_type=jnp.float32)  9.25 us
  transfers between devices with their start and end apart: 8, of which 4 were waited for; matrix products, arithmetic and copies ran while one was open for 11% of the time, Pallas kernels for 3%

profile of v1, /device:TPU:80, one launch (start us, length us, event | category | flops | bytes accessed | tf_op | source)
XLA Modules:
  0.0 306.3 jit_solution(4558615299547970357)
XLA Ops:
  6.5 0.1 pad_add_fusion.pos
  6.6 4.6 %copy.22 = bf16[8,8,16,2048]{3,2,1,0:T(8,128)(2,1)S(1)} copy(bf16[8,8,16,2048]{3,1,2,0:T(8,128)(2,1)} %bitcast.29) | data formatting | bytes 8388608
  11.2 4.3 %copy.18 = bf16[16,64,2048]{2,1,0:T(8,128)(2,1)} copy(bf16[16,64,2048]{2,0,1:T(8,128)(2,1)S(1)} %bitcast.26) | data formatting | bytes 8388608 | tf_op jit(solution)/shard_map/transpose | solution.py:28
  15.5 5.8 %all-to-all-start = ((bf16[16,64,2048]{2,1,0:T(8,128)(2,1)}), bf16[16,64,2048]{2,1,0:T(8,128)(2,1)}, u32[]{:S(2)}, u32[]{:S(2)}) async-start(bf16[16,64,2048]{2,1,0:T(8,128)(2,1)} %copy.18), calls=%async_computation | async-start | bytes 8388608 | tf_op jit(solution)/shard_map/all_to_all | solution.py:29
  21.3 0.0 all-gather.6.cloned.1.call-start
  21.3 0.7 all-gather.6.cloned.1.call-update
  22.0 0.0 all-gather.4.cloned.1.call-start
  22.1 0.7 all-gather.4.cloned.1.call-update
  22.8 4.6 %copy.23 = bf16[8,8,16,2048]{3,2,1,0:T(8,128)(2,1)S(1)} copy(bf16[8,8,16,2048]{3,1,2,0:T(8,128)(2,1)} %bitcast.30) | data formatting | bytes 8388608
  27.4 4.3 %copy.19 = bf16[16,64,2048]{2,1,0:T(8,128)(2,1)} copy(bf16[16,64,2048]{2,0,1:T(8,128)(2,1)S(1)} %bitcast.27) | data formatting | bytes 8388608 | tf_op jit(solution)/shard_map/transpose | solution.py:28
  31.6 73.7 %all-to-all-done = bf16[16,64,2048]{2,1,0:T(8,128)(2,1)} async-done(((bf16[16,64,2048]{2,1,0:T(8,128)(2,1)}), bf16[16,64,2048]{2,1,0:T(8,128)(2,1)}, u32[]{:S(2)}, u32[]{:S(2)}) %all-to-all-start) | async-done | bytes 4194336 | tf_op jit(solution)/shard_map/all_to_all | solution.py:29
  105.3 13.9 %all-to-all-start.1 = ((bf16[16,64,2048]{2,1,0:T(8,128)(2,1)}), bf16[16,64,2048]{2,1,0:T(8,128)(2,1)}, u32[]{:S(2)}, u32[]{:S(2)}) async-start(bf16[16,64,2048]{2,1,0:T(8,128)(2,1)} %copy.19), calls=%async_computation.1 | async-start | bytes 8388608 | tf_op jit(solution)/shard_map/all_to_all | solution.py:29
  119.2 0.2 all-gather.8.cloned.1.call-start
  119.4 0.5 all-gather.8.cloned.1.call-update
  119.9 3.3 %multiply_convert_fusion = bf16[16,64,2048]{2,1,0:T(8,128)(2,1)S(1)} fusion(bf16[16,64,2048]{2,1,0:T(8,128)(2,1)} %all-to-all-done, f32[2048]{0:T(1024)S(1)} %bitcast.32), kind=kLoop, calls=%fused_computation | loop fusion | flops 6291456 | bytes 8396800 | tf_op jit(solution)/shard_map/convert_element_type | solution.py:182
  123.3 8.4 %fusion = f32[1024,1024]{1,0:T(8,128)} fusion(bf16[1024,2048]{1,0:T(8,128)(2,1)} %bitcast.3, bf16[1024,2048]{1,0:T(8,128)(2,1)S(1)} %bitcast.28), kind=kOutput, calls=%fused_computation.4 | convolution fusion | flops 4294967296 | bytes 12582912 | tf_op jit(solution)/shard_map/ip,jp->ij/dot_general | solution.py:183
  131.7 67.8 %all-to-all-done.1 = bf16[16,64,2048]{2,1,0:T(8,128)(2,1)} async-done(((bf16[16,64,2048]{2,1,0:T(8,128)(2,1)}), bf16[16,64,2048]{2,1,0:T(8,128)(2,1)}, u32[]{:S(2)}, u32[]{:S(2)}) %all-to-all-start.1) | async-done | bytes 4194336 | tf_op jit(solution)/shard_map/all_to_all | solution.py:29
  199.5 9.3 %multiply_add_fusion = f32[1024,1024]{1,0:T(8,128)S(1)} fusion(f32[1024,1024]{1,0:T(8,128)} %fusion, bf16[1024,2048]{1,0:T(8,128)(2,1)} %bitcast.7), kind=kOutput, calls=%fused_computation.2 | convolution fusion | flops 4297064448 | bytes 12582912 | tf_op jit(solution)/shard_map/ip,jp->ij/dot_general | solution.py:184
  208.8 0.3 copy.25
  209.1 8.2 %all_to_all.25 = f32[2,8,64,1024]{3,2,1,0:T(8,128)} all-to-all(f32[2,8,64,1024]{3,2,1,0:T(8,128)S(1)} %bitcast.25), channel_id=1, replica_groups=mesh['y'=4,'zh'=4,'zl'=2,'x'=4,'c'=2] {'c'}, dimensions={0} | all-to-all | bytes 8388608 | tf_op jit(solution)/shard_map/all_to_all | solution.py:192
  217.3 4.4 %reduce_sum.18 = f32[8,64,1024]{2,1,0:T(8,128)} reduce(f32[2,8,64,1024]{3,2,1,0:T(8,128)} %all_to_all.25, f32[]{:T(128)} %constant.19.clone.1), dimensions={0}, to_apply=%region_0.0 | reduce | flops 524288 | bytes 6291460 | tf_op jit(solution)/shard_map/reduce_sum | solution.py:192
  221.6 3.7 %all-to-all-start.3 = ((f32[8,64,1024]{2,1,0:T(8,128)}), f32[8,64,1024]{2,1,0:T(8,128)S(1)}, u32[]{:S(2)}, u32[]{:S(2)}) async-start(f32[8,64,1024]{2,1,0:T(8,128)} %reduce_sum.18), calls=%async_computation.3 | async-start | bytes 4194304 | tf_op jit(solution)/shard_map/all_to_all | solution.py:193
  225.4 0.2 collective-permute-start.1
  225.6 26.3 %all-to-all-done.3 = f32[8,64,1024]{2,1,0:T(8,128)S(1)} async-done(((f32[8,64,1024]{2,1,0:T(8,128)}), f32[8,64,1024]{2,1,0:T(8,128)S(1)}, u32[]{:S(2)}, u32[]{:S(2)}) %all-to-all-start.3) | async-done | bytes 2097184 | tf_op jit(solution)/shard_map/all_to_all | solution.py:193
  251.9 0.1 reduce_sum.19
  252.1 0.1 broadcast_in_dim.2
  252.2 19.4 %all_to_all.26.mine_ref = bf16[8,64,1024]{2,1,0:T(8,128)(2,1)S(1)} all-to-all(bf16[8,64,1024]{2,1,0:T(8,128)(2,1)S(1)} %broadcast_in_dim.2), channel_id=1, replica_groups=mesh['y'=4,'zh'=4,'zl'=2,'x'=4,'c'=2] {'zl','x'}, dimensions={0} | all-to-all | bytes 2097152 | tf_op jit(solution)/shard_map/all_to_all | solution.py:20
  271.6 0.1 copy.21.near
  271.7 14.0 %all-gather.8.cloned.1.call-done.refs_0_.refs_1_.refs_2_.refs_3_ = bf16[16,1024,256]{2,1,0:T(8,128)(2,1)} async-done(((bf16[4,1024,256]{2,1,0:T(8,128)(2,1)}), bf16[16,1024,256]{2,1,0:T(8,128)(2,1)}) %all-gather.8.cloned.1.call-update) | async-done | bytes 8388624 | tf_op jit(solution)/shard_map/all_gather | solution.py:178
  285.7 2.2 copy-done
  287.9 9.4 %hop_apply.1.h_ref = f32[8,2,64,256]{3,2,1,0:T(8,128)S(1)} custom-call(s32[2]{0:T(128)S(1)} %pad_add_fusion.pos, s32[16]{0:T(128)S(1)} %copy-done.2, s32[16,4]{1,0:T(8,128)S(1)} %copy.21.near, bf16[8,4,64,1024]{3,2,1,0:T(8,128)(2,1)S(1)} %copy-done, bf16[8,4,64,1024]{3,2,1,0:T(8,128)(2,1)} %collective-permute-done.1.other_ref, ...), custom_call_target="tpu_custom_call" | custom-call | flops 2147483648 | bytes 10485760 | tf_op jit(solution)/shard_map/hop_apply/pallas_call | solution.py:84
  297.3 2.5 own_apply.1
  (14 shorter events, 0.1 us)
Async XLA Ops:
  15.5 89.9 %all-to-all-start = ((bf16[16,64,2048]{2,1,0:T(8,128)(2,1)}), bf16[16,64,2048]{2,1,0:T(8,128)(2,1)}, u32[]{:S(2)}, u32[]{:S(2)}) async-start(bf16[16,64,2048]{2,1,0:T(8,128)(2,1)} %copy.18), calls=%async_computation | async-start | bytes 8388608 | tf_op jit(solution)/shard_map/all_to_all | solution.py:29
  21.3 98.2 %all-gather.6.cloned.1.call-start = ((), (), s32[]{:S(2)}) async-start(), calls=%async_computation.6 | async-start | bytes 2621440 | tf_op jit(solution)/shard_map/all_gather | solution.py:177
  22.0 203.4 %all-gather.4.cloned.1.call-start = ((), (), s32[]{:S(2)}) async-start(), calls=%async_computation.5 | async-start | bytes 4718592 | tf_op jit(solution)/shard_map/all_gather | solution.py:179
  31.6 88.3 %copy-start.3 = (f32[1,2048]{1,0:T(1,128)S(1)}, f32[1,2048]{1,0:T(1,128)}, u32[]{:S(2)}) copy-start(f32[1,2048]{1,0:T(1,128)} %param.9) | copy-start | bytes 24580
  105.3 94.2 %all-to-all-start.1 = ((bf16[16,64,2048]{2,1,0:T(8,128)(2,1)}), bf16[16,64,2048]{2,1,0:T(8,128)(2,1)}, u32[]{:S(2)}, u32[]{:S(2)}) async-start(bf16[16,64,2048]{2,1,0:T(8,128)(2,1)} %copy.19), calls=%async_computation.1 | async-start | bytes 8388608 | tf_op jit(solution)/shard_map/all_to_all | solution.py:29
  119.2 166.5 %all-gather.8.cloned.1.call-start = ((), (), s32[]{:S(2)}) async-start(), calls=%async_computation.7 | async-start | bytes 10485760 | tf_op jit(solution)/shard_map/all_gather | solution.py:178
  221.6 50.0 %copy-start.4 = (s32[16,4]{0,1:T(4,128)S(1)}, s32[16,4]{0,1:T(4,128)}, u32[]{:S(2)}) copy-start(s32[16,4]{0,1:T(4,128)} %param.13) | copy-start | bytes 772
  221.6 64.0 %copy-start.2 = (s32[16]{0:T(128)S(1)}, s32[16]{0:T(128)}, u32[]{:S(2)}) copy-start(s32[16]{0:T(128)} %counts.3) | copy-start | bytes 196
  221.6 30.3 %all-to-all-start.3 = ((f32[8,64,1024]{2,1,0:T(8,128)}), f32[8,64,1024]{2,1,0:T(8,128)S(1)}, u32[]{:S(2)}, u32[]{:S(2)}) async-start(f32[8,64,1024]{2,1,0:T(8,128)} %reduce_sum.18), calls=%async_computation.3 | async-start | bytes 4194304 | tf_op jit(solution)/shard_map/all_to_all | solution.py:193
  225.4 46.3 %collective-permute-start.1 = (bf16[8,4,64,1024]{3,2,1,0:T(8,128)(2,1)}, bf16[8,4,64,1024]{3,2,1,0:T(8,128)(2,1)}, u32[]{:S(2)}, u32[]{:S(2)}) collective-permute-start(bf16[8,4,64,1024]{3,2,1,0:T(8,128)(2,1)} %all-gather.4.cloned.1.call-done.mine_ref), channel_id=1, source_target_pairs={{0,1},{1,0},{2,3},{3,2},{4,5},{5,4},{6,7},{7,6},{8,9},{9,8},{10,11... | collective-permute-start | bytes 12582920 | tf_op jit(solution)/shard_map/ppermute | solution.py:15
  271.6 25.7 %collective-permute-start = (bf16[8,64,1024]{2,1,0:T(8,128)(2,1)S(1)}, bf16[8,64,1024]{2,1,0:T(8,128)(2,1)S(1)}, u32[]{:S(2)}, u32[]{:S(2)}) collective-permute-start(bf16[8,64,1024]{2,1,0:T(8,128)(2,1)S(1)} %all_to_all.26.mine_ref), channel_id=1, source_target_pairs={{0,1},{1,0},{2,3},{3,2},{4,5},{5,4},{6,7},{7,6},{8,9},{9,8},{10,11... | collective-permute-start | bytes 3145736 | tf_op jit(solution)/shard_map/ppermute | solution.py:15
  285.7 2.2 copy-start
  287.8 9.4 %copy-start.1 = (bf16[1,1024,256]{2,1,0:T(8,128)(2,1)S(1)}, bf16[1,1024,256]{2,1,0:T(8,128)(2,1)}, u32[]{:S(2)}) copy-start(bf16[1,1024,256]{2,1,0:T(8,128)(2,1)} %x_ref.1) | copy-start | bytes 1572868
Sparse Core Ops, SparseCore 0:
  23.9 66.5 all-gather.5
  92.3 106.1 all-gather.3
  200.3 85.3 all-gather.7

commit v2 on v0

v2 whole, which is shorter than its diff:
```python
import jax
import jax.numpy as jnp
from jax import lax
from jax.experimental import pallas as pl
from jax.experimental.pallas import tpu as pltpu
from jax.sharding import Mesh, PartitionSpec as P

ELEM = ("y", "zh")
CHIPS = ("zl", "x")
GRP = ("zl", "x", "c")
CORES = 2
SIDE = 4


def swap_cores(a):
    return lax.ppermute(a, "c", [(0, 1), (1, 0)])


def shift(a, axis, step):
    size = lax.axis_size(axis)
    return lax.ppermute(a, axis, [((i + step) % size, i) for i in range(size)])


def far(after, before, axis):
    size = lax.axis_size(axis)
    held = jnp.where(lax.axis_index("c") == 0, after, before)
    pairs = []
    for i in range(size):
        pairs.append((((i + 1) % size) * CORES, i * CORES))
        pairs.append((((i - 1) % size) * CORES + 1, i * CORES + 1))
    return lax.ppermute(held, (axis, "c"), pairs)


def split_kernel(a_ref, o_ref, sems):
    devices, _, points = o_ref.shape
    copies = [
        pltpu.make_async_copy(a_ref.at[:, pl.ds(i * points, points)], o_ref.at[i], sems.at[i])
        for i in range(devices)
    ]
    for copy in copies:
        copy.start()
    for copy in copies:
        copy.wait()


def split_points(a):
    rows, points = a.shape
    devices = lax.axis_size(GRP)
    return pl.pallas_call(
        split_kernel,
        out_shape=jax.ShapeDtypeStruct((devices, rows, points // devices), a.dtype),
        in_specs=[pl.BlockSpec(memory_space=pltpu.HBM)],
        out_specs=pl.BlockSpec(memory_space=pltpu.VMEM),
        scratch_shapes=[pltpu.SemaphoreType.DMA((devices,))],
        cost_estimate=pl.CostEstimate(flops=0, bytes_accessed=4 * a.size, transcendentals=0),
        name="split_points",
    )(a)


def triangle(side):
    return [j * (j + 1) // 2 for j in range(side)]


def value_kernel(p_ref, v_ref, o_ref):
    size = o_ref.shape[1]
    for j, first in enumerate(triangle(SIDE)):
        v = v_ref[pl.ds(j * size, size), :].astype(jnp.float32)
        w = (p_ref[...] * v).astype(jnp.bfloat16)
        d = lax.dot_general(
            v_ref[pl.ds(0, (j + 1) * size), :],
            w,
            (((1,), (1,)), ((), ())),
            preferred_element_type=jnp.float32,
        )
        o_ref[pl.ds(first, j + 1)] = d.reshape(j + 1, size, size)


def value_part(potential, values):
    rows, points = values.shape
    size = rows // SIDE
    blocks = SIDE * (SIDE + 1) // 2
    return pl.pallas_call(
        value_kernel,
        out_shape=jax.ShapeDtypeStruct((blocks, size, size), jnp.float32),
        compiler_params=pltpu.CompilerParams(vmem_limit_bytes=40 << 20),
        cost_estimate=pl.CostEstimate(
            flops=2 * blocks * size * size * points,
            bytes_accessed=2 * values.size + 4 * blocks * size * size,
            transcendentals=0,
        ),
        name="value_part",
    )(potential, values)


def deriv_kernel(pos, d_ref, g_ref, keep_ref, send_ref):
    size = g_ref.shape[1]
    half = size // CORES
    first_core = pos[0] == 0
    for j, first in enumerate(triangle(SIDE)):
        d = lax.dot_general(
            d_ref[pl.ds(0, (j + 1) * size), :],
            d_ref[pl.ds(j * size, size), :],
            (((1,), (1,)), ((), ())),
            preferred_element_type=jnp.float32,
        )
        d = 0.5 * d.reshape(j + 1, size, size) + g_ref[pl.ds(first, j + 1)]
        top, bottom = d[:, :half], d[:, half:]
        for ref, part in (
            (keep_ref, jnp.where(first_core, top, bottom)),
            (send_ref, jnp.where(first_core, bottom, top)),
        ):
            chips, _, rows, _ = ref.shape
            part = part.reshape(j + 1, chips, rows, size)
            for i in range(j + 1):
                ref[:, first + i] = part[i]


def deriv_part(pos, derivs, partial):
    blocks, size, _ = partial.shape
    chips = lax.axis_size(CHIPS)
    out = jax.ShapeDtypeStruct((chips, blocks, size // CORES // chips, size), jnp.float32)
    vmem = pl.BlockSpec(memory_space=pltpu.VMEM)
    return pl.pallas_call(
        deriv_kernel,
        out_shape=(out, out),
        in_specs=[pl.BlockSpec(memory_space=pltpu.SMEM), vmem, vmem],
        compiler_params=pltpu.CompilerParams(vmem_limit_bytes=40 << 20),
        cost_estimate=pl.CostEstimate(
            flops=2 * partial.size * derivs.shape[1],
            bytes_accessed=2 * derivs.size + 8 * partial.size,
            transcendentals=0,
        ),
        name="deriv_part",
    )(pos, derivs, partial)


def masked_copy(src, count):
    rows = lax.broadcasted_iota(jnp.int32, src.shape, 0)
    src = src.astype(jnp.float32)
    return jnp.where(rows < count, src, jnp.zeros_like(src)).astype(jnp.bfloat16)


def hop_places(pos):
    places = []
    for core in (pos[0], 1 - pos[0]):
        for dx in (0, 1, 3, 2):
            for zl in (pos[4], 1 - pos[4]):
                places.append((zl * 4 + ((pos[5] + dx) & 3)) * CORES + core)
    return places


def hop_kernel(pos, counts, near, *refs):
    hop_refs, piece_refs = refs[:16], refs[16:-5]
    o_ref, hops, near_coeffs, hop_sem, near_sem = refs[-5:]
    many, _, rows, width = hops.shape
    places = hop_places(pos)
    copies = [
        pltpu.make_async_copy(ref.at[0], hops.at[:, places[i]], hop_sem.at[i])
        for i, ref in enumerate(hop_refs)
    ]
    for copy in copies:
        copy.start()
    stacked, opposite = piece_refs[:4], piece_refs[4:]
    for k in range(many):
        element = near[pos[1], k]
        dy = ((element >> 2) - pos[2]) & 3
        dz = ((element & 3) - pos[3]) & 3
        for z in range(4):
            for y in range(4):
                piece = opposite[y].at[0] if z == 2 else stacked[y].at[(0, 1, 0, 2)[z]]

                @pl.when((dz == z) & (dy == y))
                def _():
                    pltpu.make_async_copy(piece, near_coeffs.at[k], near_sem.at[k]).start()

    for copy in copies:
        copy.wait()
    for k in range(many):
        pltpu.make_async_copy(piece_refs[0].at[0], near_coeffs.at[k], near_sem.at[k]).wait()
        x = masked_copy(near_coeffs[k], counts[near[pos[1], k]])
        part = jnp.dot(hops[k].reshape(-1, width), x, preferred_element_type=jnp.float32)
        if k == 0:
            o_ref[...] = part
        else:
            o_ref[...] += part


def hop_apply(pos, counts, near, hops, pieces):
    _, many, rows, width = hops[0].shape
    blocks = len(hops)
    bands = pieces[0].shape[2]
    smem = pl.BlockSpec(memory_space=pltpu.SMEM)
    return pl.pallas_call(
        hop_kernel,
        out_shape=jax.ShapeDtypeStruct((blocks * rows, bands), jnp.float32),
        in_specs=[smem] * 3 + [pl.BlockSpec(memory_space=pltpu.HBM)] * (len(hops) + len(pieces)),
        scratch_shapes=[
            pltpu.VMEM((many, blocks, rows, width), jnp.bfloat16),
            pltpu.VMEM((many, width, bands), jnp.bfloat16),
            pltpu.SemaphoreType.DMA((blocks,)),
            pltpu.SemaphoreType.DMA((many,)),
        ],
        compiler_params=pltpu.CompilerParams(vmem_limit_bytes=60 << 20),
        cost_estimate=pl.CostEstimate(
            flops=2 * len(hops) * hops[0].size * bands,
            bytes_accessed=2 * len(hops) * hops[0].size + 2 * many * width * bands,
            transcendentals=0,
        ),
        name="hop_apply",
    )(pos, counts, near, *hops, *pieces)


def own_kernel(pos, counts, mine_ref, other_ref, x_ref, h_ref, o_ref, low):
    chips, blocks, rows, size = mine_ref.shape
    half = size // CORES
    for ref, core in ((mine_ref, pos[0]), (other_ref, 1 - pos[0])):
        at = pl.multiple_of(core * half, half)
        for g in range(chips):
            low[:, pl.ds(at + g * rows, rows), :] = ref[g]
    count = counts[pos[1]]
    x = masked_copy(x_ref[0], count)
    o_ref[...] = h_ref[...]
    for j, first in enumerate(triangle(SIDE)):
        column = low[pl.ds(first, j + 1)].reshape((j + 1) * size, size)
        here = pl.ds(j * size, size)
        o_ref[pl.ds(0, (j + 1) * size), :] += jnp.dot(
            column, x[j * size : (j + 1) * size], preferred_element_type=jnp.float32
        )
        if j:
            o_ref[here, :] += lax.dot_general(
                column[: j * size],
                x[: j * size],
                (((0,), (0,)), ((), ())),
                preferred_element_type=jnp.float32,
            )
    at = lax.broadcasted_iota(jnp.int32, o_ref.shape, 0)
    o_ref[...] = jnp.where(at < count, o_ref[...], jnp.zeros_like(o_ref))


def own_apply(pos, counts, mine, other, coeffs, hopped):
    chips, blocks, rows, size = mine.shape
    smem, vmem = pl.BlockSpec(memory_space=pltpu.SMEM), pl.BlockSpec(memory_space=pltpu.VMEM)
    return pl.pallas_call(
        own_kernel,
        out_shape=jax.ShapeDtypeStruct(hopped.shape, jnp.float32),
        in_specs=[smem, smem] + [vmem] * 4,
        scratch_shapes=[pltpu.VMEM((blocks, size, size), jnp.bfloat16)],
        compiler_params=pltpu.CompilerParams(vmem_limit_bytes=40 << 20),
        cost_estimate=pl.CostEstimate(
            flops=2 * coeffs.shape[1] ** 2 * coeffs.shape[2],
            bytes_accessed=4 * mine.size + 2 * coeffs.size + 8 * hopped.size,
            transcendentals=0,
        ),
        name="own_apply",
    )(pos, counts, mine, other, coeffs, hopped)


def local(basis_values, basis_derivs, potential, hop_blocks, coeffs, counts, neighbours):
    pos = [lax.axis_index(n) for n in ("c", ELEM, "y", "zh", "zl", "x")]
    pos = jnp.stack(pos).astype(jnp.int32)
    basis_values, pos = lax.optimization_barrier((basis_values, pos))

    def exchange(a):
        return lax.all_to_all(a, GRP, 0, 0, tiled=True)

    barrier = lax.optimization_barrier
    pair = shift(hop_blocks, "zl", 1)
    own_x = [shift(hop_blocks, "x", 1), shift(hop_blocks, "x", 3)]
    pair, own_x, ring = barrier((pair, own_x, coeffs))
    after, before = shift(ring, "zh", 1), shift(ring, "zh", 3)
    pair_x = [shift(pair, "x", 1), shift(pair, "x", 3)]
    own_far = far(*own_x, "x")
    values, after, before, pair_x, own_far = barrier(
        (split_points(basis_values[0]), after, before, pair_x, own_far)
    )

    values = exchange(values)
    stacked = jnp.concatenate([coeffs, after, before])
    opposite = far(after, before, "zh")
    near_y = [shift(stacked, "y", 1), shift(stacked, "y", 3)]
    pair_far = far(*pair_x, "x")
    derivs, opposite, near_y, pair_far = barrier(
        (split_points(basis_derivs[0]), opposite, near_y, pair_far)
    )

    derivs = exchange(derivs)
    far_y = far(*near_y, "y")
    near_o = [shift(opposite, "y", 1), shift(opposite, "y", 3)]
    pieces = [stacked, near_y[0], far_y, near_y[1]]
    pieces += [opposite, near_o[0], far(*near_o, "y"), near_o[1]]
    hops = [hop_blocks, pair, own_x[0], pair_x[0], own_x[1], pair_x[1], own_far, pair_far]
    others = [swap_cores(h) for h in hops]
    hopped = hop_apply(pos, counts, neighbours, hops + others, pieces)
    width = coeffs.shape[1]
    part = value_part(potential, values.reshape(width, -1))
    derivs, hopped, part = barrier((derivs, hopped, part))

    keep, send = deriv_part(pos, derivs.reshape(width, -1), part)
    part = keep + swap_cores(send)
    part = lax.all_to_all(part, CHIPS, 0, 0, tiled=True).sum(0).astype(jnp.bfloat16)
    chips = lax.axis_size(CHIPS)
    low = jnp.broadcast_to(part[None], (chips, *part.shape))
    low = lax.all_to_all(low, CHIPS, 0, 0, tiled=True)
    result = own_apply(pos, counts, low, swap_cores(low), coeffs, hopped)
    return result[None]


def solution(mesh):
    fine = Mesh(mesh.devices.reshape(4, 4, 2, 4, 2), ("y", "zh", "zl", "x", "c"))
    placed = (
        P(ELEM, GRP, None),
        P(ELEM, GRP, None),
        P(ELEM, GRP),
        P(ELEM, None, GRP, None),
        P(ELEM, None, GRP),
        P(),
        P(),
    )
    return jax.shard_map(
        local, mesh=fine, in_specs=placed, out_specs=P(ELEM, None, GRP), check_vma=False
    )
```

time: 714 us -> 243 us (0.34); the launches traced: 702 us -> 240 us
  other arithmetic: 363 us -> 7.78 us
  local copies, waits for them, and re-layouts: 214 us -> 8.11 us
  waiting for transfers between devices: 0.45 us -> 103 us
  blocking collectives: 78.7 us -> 43.7 us
  starting transfers between devices: 12.6 us -> 44.9 us
  Pallas kernels: 0 us -> 31.9 us
  matrix products: 19.1 us -> 0 us
  between operations: 13.8 us -> 0.23 us
    unnamed x2 -> x0, other arithmetic: 358 us -> none
    unnamed x17 -> x55, local copies, waits for them, and re-layouts: 133 us -> 7.41 us
    ppermute x0 -> x26, waiting for transfers between devices: none -> 94.2 us  [the longest x5 51.8 us: far(): return lax.ppermute(held, (axis, 'c'), pairs)]
    psum x1 -> x0, blocking collectives: 78.7 us -> none  [local(): assembled_low = lax.psum(partial_value, 'grp').astype(jnp.bfloat16)]
    all_to_all x6 -> x0, local copies, waits for them, and re-layouts: 72.1 us -> none  [the longest x3 37 us: local(): lax.all_to_all(basis_derivs, 'grp', split_axis=2, concat_axis=1, tiled=True)]
    all_to_all x0 -> x2, blocking collectives: none -> 43.7 us  [the longest x1 29.4 us: local(): lax.all_to_all(part, CHIPS, 0, 0, tiled=True).sum(0).astype(jnp.bfloat16)]
    pallas_call x0 -> x6, Pallas kernels: none -> 31.9 us  [the longest x1 10.7 us: hop_apply(): pl.pallas_call(hop_kernel, out_shape=jax.ShapeDtypeStruct((blocks * rows,...]
    ppermute x0 -> x26, starting transfers between devices: none -> 24.6 us  [the longest x11 16.7 us: shift(): return lax.ppermute(a, axis, [((i + step) % size, i) for i in range(size)])]
  transfers between devices with their start and end apart: 4 -> 28, of which waited for: 0 -> 15; matrix products, arithmetic and copies ran while one was open for 83% -> 4% of each run, Pallas kernels for 0% -> 10%
where the time goes in v2:
time: 243 us; the launch traced here: 240 us
  waiting for transfers between devices  103 us (42%)
  starting transfers between devices  44.9 us (18%)
  blocking collectives  43.7 us (18%)
  Pallas kernels  31.9 us (13%)
  local copies, waits for them, and re-layouts  8.11 us (3%)
  other arithmetic  7.78 us (3%)
    ppermute x5, waiting for transfers between devices, far(): return lax.ppermute(held, (axis, 'c'), pairs)  51.8 us
    ppermute x11, waiting for transfers between devices, shift(): return lax.ppermute(a, axis, [((i + step) % size, i) for i in range(size)])  36.6 us
    all_to_all x1, blocking collectives, local(): lax.all_to_all(part, CHIPS, 0, 0, tiled=True).sum(0).astype(jnp.bfloat16)  29.4 us
    all_to_all x2, starting transfers between devices, exchange(): return lax.all_to_all(a, GRP, 0, 0, tiled=True)  20.3 us
    ppermute x11, starting transfers between devices, shift(): return lax.ppermute(a, axis, [((i + step) % size, i) for i in range(size)])  16.7 us
    all_to_all x1, blocking collectives, local(): low = lax.all_to_all(low, CHIPS, 0, 0, tiled=True)  14.3 us
    pallas_call x1, Pallas kernels, hop_apply(): pl.pallas_call(hop_kernel, out_shape=jax.ShapeDtypeStruct((blocks * rows,...  10.7 us
    all_to_all x2, waiting for transfers between devices, exchange(): return lax.all_to_all(a, GRP, 0, 0, tiled=True)  8.77 us
  transfers between devices with their start and end apart: 28, of which 15 were waited for; matrix products, arithmetic and copies ran while one was open for 4% of the time, Pallas kernels for 10%

profile of v2, /device:TPU:80, one launch (start us, length us, event | category | flops | bytes accessed | tf_op | source)
XLA Modules:
  0.0 239.6 jit_solution(9458259877009533874)
XLA Ops:
  0.0 1.5 collective-permute-start.2
  1.5 1.7 collective-permute-start.1
  3.2 1.9 collective-permute-start
  5.2 9.9 %collective-permute-done.2.refs_4_ = bf16[1,4,64,1024]{3,2,1,0:T(8,128)(2,1)S(1)} collective-permute-done((bf16[1,4,64,1024]{3,2,1,0:T(8,128)(2,1)}, bf16[1,4,64,1024]{3,2,1,0:T(8,128)(2,1)S(1)}, u32[]{:S(2)}, u32[]{:S(2)}) %collective-permute-start.2) | collective-permute-done | bytes 524320 | tf_op jit(solution)/shard_map/ppermute | solution.py:21
  15.1 1.8 collective-permute-done.refs_1_
  17.7 1.5 collective-permute-start.7
  19.3 4.3 %collective-permute-start.4 = (bf16[1,1024,256]{2,1,0:T(8,128)(2,1)S(1)}, bf16[1,1024,256]{2,1,0:T(8,128)(2,1)}, u32[]{:S(2)}, u32[]{:S(2)}) collective-permute-start(bf16[1,1024,256]{2,1,0:T(8,128)(2,1)S(1)} %copy-done.1), channel_id=1, source_target_pairs={{48,0},{0,16},{16,32},{32,48},{49,1},{1,17},{17,33},{33,49},{50,2}... | collective-permute-start | bytes 1572872 | tf_op jit(solution)/shard_map/ppermute | solution.py:21
  24.0 2.8 %collective-permute-start.5 = (bf16[1,4,64,1024]{3,2,1,0:T(8,128)(2,1)}, bf16[1,4,64,1024]{3,2,1,0:T(8,128)(2,1)S(1)}, u32[]{:S(2)}, u32[]{:S(2)}) collective-permute-start(bf16[1,4,64,1024]{3,2,1,0:T(8,128)(2,1)} %collective-permute-done.refs_1_), channel_id=1, source_target_pairs={{2,0},{4,2},{6,4},{0,6},{3,1},{5,3},{7,5},{1,7},{10,8},{12,10},{14... | collective-permute-start | bytes 1572872 | tf_op jit(solution)/shard_map/ppermute | solution.py:21
  27.4 4.3 %split_points.3 = bf16[16,64,2048]{2,1,0:T(8,128)(2,1)} custom-call(bf16[64,32768]{1,0:T(8,128)(2,1)} %bitcast.11), custom_call_target="tpu_custom_call" | custom-call | bytes 8388608 | tf_op jit(solution)/shard_map/split_points/pallas_call | solution.py:49
  31.8 11.2 %collective-permute-done.4 = bf16[1,1024,256]{2,1,0:T(8,128)(2,1)} collective-permute-done((bf16[1,1024,256]{2,1,0:T(8,128)(2,1)S(1)}, bf16[1,1024,256]{2,1,0:T(8,128)(2,1)}, u32[]{:S(2)}, u32[]{:S(2)}) %collective-permute-start.4) | collective-permute-done | bytes 524320 | tf_op jit(solution)/shard_map/ppermute | solution.py:21
  43.0 4.2 %collective-permute-done.3 = bf16[1,1024,256]{2,1,0:T(8,128)(2,1)S(1)} collective-permute-done((bf16[1,1024,256]{2,1,0:T(8,128)(2,1)S(1)}, bf16[1,1024,256]{2,1,0:T(8,128)(2,1)S(1)}, u32[]{:S(2)}, u32[]{:S(2)}) %collective-permute-start.3) | collective-permute-done | bytes 524320 | tf_op jit(solution)/shard_map/ppermute | solution.py:21
  48.2 4.5 %all-to-all-start.1 = ((bf16[16,64,2048]{2,1,0:T(8,128)(2,1)}), bf16[16,64,2048]{2,1,0:T(8,128)(2,1)}, u32[]{:S(2)}, u32[]{:S(2)}) async-start(bf16[16,64,2048]{2,1,0:T(8,128)(2,1)} %split_points.3), calls=%async_computation.1 | async-start | bytes 8388608 | tf_op jit(solution)/shard_map/all_to_all | solution.py:264
  54.4 2.1 constant_dynamic-update-slice_fusion
  56.5 1.3 collective-permute-start.10
  59.4 3.0 %collective-permute-start.11 = (bf16[1,4,64,1024]{3,2,1,0:T(8,128)(2,1)}, bf16[1,4,64,1024]{3,2,1,0:T(8,128)(2,1)}, u32[]{:S(2)}, u32[]{:S(2)}) collective-permute-start(bf16[1,4,64,1024]{3,2,1,0:T(8,128)(2,1)} %broadcast_select_fusion.1), channel_id=1, source_target_pairs={{2,0},{7,1},{4,2},{1,3},{6,4},{3,5},{0,6},{5,7},{10,8},{15,9},{12,... | collective-permute-start | bytes 1572872 | tf_op jit(solution)/shard_map/ppermute | solution.py:31
  62.4 4.3 %split_points.2 = bf16[16,64,2048]{2,1,0:T(8,128)(2,1)} custom-call(bf16[64,32768]{1,0:T(8,128)(2,1)} %bitcast.12), custom_call_target="tpu_custom_call" | custom-call | bytes 8388608 | tf_op jit(solution)/shard_map/split_points/pallas_call | solution.py:49
  66.7 34.2 %collective-permute-done.11.refs_7_ = bf16[1,4,64,1024]{3,2,1,0:T(8,128)(2,1)} collective-permute-done((bf16[1,4,64,1024]{3,2,1,0:T(8,128)(2,1)}, bf16[1,4,64,1024]{3,2,1,0:T(8,128)(2,1)}, u32[]{:S(2)}, u32[]{:S(2)}) %collective-permute-start.11) | collective-permute-done | bytes 524320 | tf_op jit(solution)/shard_map/ppermute | solution.py:31
  100.9 8.1 %all-to-all-done.1 = bf16[16,64,2048]{2,1,0:T(8,128)(2,1)} async-done(((bf16[16,64,2048]{2,1,0:T(8,128)(2,1)}), bf16[16,64,2048]{2,1,0:T(8,128)(2,1)}, u32[]{:S(2)}, u32[]{:S(2)}) %all-to-all-start.1) | async-done | bytes 4194336 | tf_op jit(solution)/shard_map/all_to_all | solution.py:264
  109.0 15.8 %all-to-all-start = ((bf16[16,64,2048]{2,1,0:T(8,128)(2,1)}), bf16[16,64,2048]{2,1,0:T(8,128)(2,1)}, u32[]{:S(2)}, u32[]{:S(2)}) async-start(bf16[16,64,2048]{2,1,0:T(8,128)(2,1)} %split_points.2), calls=%async_computation | async-start | bytes 8388608 | tf_op jit(solution)/shard_map/all_to_all | solution.py:264
  127.1 2.7 %broadcast_select_fusion = bf16[3,1024,256]{2,1,0:T(8,128)(2,1)} fusion(bf16[3,1024,256]{2,1,0:T(8,128)(2,1)} %collective-permute-done.9.refs_17_, bf16[3,1024,256]{2,1,0:T(8,128)(2,1)S(1)} %collective-permute-done.10.refs_19_, pred[]{:T(512)S(6)} %eq.2), kind=kLoop, calls=%fused_computation | loop fusion | flops 786432 | bytes 4718593 | tf_op jit(solution)/shard_map/jit(_where)/select_n | solution.py:26
  130.9 9.2 %collective-permute-done.22.refs_23_ = bf16[1,1024,256]{2,1,0:T(8,128)(2,1)S(1)} collective-permute-done((bf16[1,1024,256]{2,1,0:T(8,128)(2,1)}, bf16[1,1024,256]{2,1,0:T(8,128)(2,1)S(1)}, u32[]{:S(2)}, u32[]{:S(2)}) %collective-permute-start.22) | collective-permute-done | bytes 524320 | tf_op jit(solution)/shard_map/ppermute | solution.py:21
  145.3 17.6 %collective-permute-done.23.refs_22_ = bf16[1,1024,256]{2,1,0:T(8,128)(2,1)} collective-permute-done((bf16[1,1024,256]{2,1,0:T(8,128)(2,1)}, bf16[1,1024,256]{2,1,0:T(8,128)(2,1)}, u32[]{:S(2)}, u32[]{:S(2)}) %collective-permute-start.23) | collective-permute-done | bytes 524320 | tf_op jit(solution)/shard_map/ppermute | solution.py:31
  163.0 10.7 %hop_apply.1.h_ref = f32[1024,256]{1,0:T(8,128)} custom-call(s32[6]{0:T(128)} %stack.27.pos, s32[16]{0:T(128)} %counts.3, s32[16,4]{1,0:T(8,128)} %copy.8.near, bf16[1,4,64,1024]{3,2,1,0:T(8,128)(2,1)} %refs_0_.1, bf16[1,4,64,1024]{3,2,1,0:T(8,128)(2,1)} %collective-permute-done.refs_1_, bf16[1,4,64,1024]{3,2,1,0:T(8,128)(2,1)} %copy-done.9, ...), custom_call_target="tpu_custom_call" | custom-call | flops 2147483648 | bytes 10485760 | tf_op jit(solution)/shard_map/hop_apply/pallas_call | solution.py:193
  173.7 5.1 %value_part.1.g_ref = f32[10,256,256]{2,1,0:T(8,128)S(1)} custom-call(f32[1,2048]{1,0:T(1,128)S(1)} %copy-done.4, bf16[1024,2048]{1,0:T(8,128)(2,1)} %bitcast.8.v_ref), custom_call_target="tpu_custom_call" | custom-call | flops 2684354560 | bytes 6815744 | tf_op jit(solution)/shard_map/value_part/pallas_call | solution.py:82
  178.8 1.5 copy-done.5
  181.0 1.7 copy-done.6
  182.7 5.1 %deriv_part.1 = (f32[8,10,16,256]{3,2,1,0:T(8,128)S(1)}, f32[8,10,16,256]{3,2,1,0:T(8,128)S(1)}) custom-call(s32[6]{0:T(128)S(1)} %copy-done.2, bf16[1024,2048]{1,0:T(8,128)(2,1)} %bitcast.9.d_ref, f32[10,256,256]{2,1,0:T(8,128)S(1)} %copy-done.6), custom_call_target="tpu_custom_call" | custom-call | flops 2684354560 | bytes 9437184 | tf_op jit(solution)/shard_map/deriv_part/pallas_call | solution.py:123
  187.9 3.0 %collective-permute-done.24 = f32[8,10,16,256]{3,2,1,0:T(8,128)S(1)} collective-permute-done((f32[8,10,16,256]{3,2,1,0:T(8,128)S(1)}, f32[8,10,16,256]{3,2,1,0:T(8,128)S(1)}, u32[]{:S(2)}, u32[]{:S(2)}) %collective-permute-start.24) | collective-permute-done | bytes 1310752 | tf_op jit(solution)/shard_map/ppermute | solution.py:16
  191.2 29.4 %all_to_all.20 = f32[8,10,16,256]{3,2,1,0:T(8,128)S(1)} all-to-all(f32[8,10,16,256]{3,2,1,0:T(8,128)S(1)} %add.7), channel_id=1, replica_groups=mesh['y'=4,'zh'=4,'zl'=2,'x'=4,'c'=2] {'zl','x'}, dimensions={0} | all-to-all | bytes 2621440 | tf_op jit(solution)/shard_map/all_to_all | solution.py:300
  220.8 14.3 %all_to_all.21.mine_ref = bf16[8,10,16,256]{3,2,1,0:T(8,128)(2,1)S(1)} all-to-all(bf16[8,10,16,256]{3,2,1,0:T(8,128)(2,1)S(1)} %broadcast_in_dim.4), channel_id=1, replica_groups=mesh['y'=4,'zh'=4,'zl'=2,'x'=4,'c'=2] {'zl','x'}, dimensions={0} | all-to-all | bytes 1310720 | tf_op jit(solution)/shard_map/all_to_all | solution.py:303
  235.1 2.1 collective-permute-done.25.other_ref
  237.2 2.3 own_apply.1
  (96 shorter events, 16.1 us)
Async XLA Ops:
  0.0 15.1 %collective-permute-start.2 = (bf16[1,4,64,1024]{3,2,1,0:T(8,128)(2,1)}, bf16[1,4,64,1024]{3,2,1,0:T(8,128)(2,1)S(1)}, u32[]{:S(2)}, u32[]{:S(2)}) collective-permute-start(bf16[1,4,64,1024]{3,2,1,0:T(8,128)(2,1)} %refs_0_.1), channel_id=1, source_target_pairs={{6,0},{0,2},{2,4},{4,6},{7,1},{1,3},{3,5},{5,7},{14,8},{8,10},{10,... | collective-permute-start | bytes 1572872 | tf_op jit(solution)/shard_map/ppermute | solution.py:21
  1.5 13.6 %collective-permute-start.1 = (bf16[1,4,64,1024]{3,2,1,0:T(8,128)(2,1)}, bf16[1,4,64,1024]{3,2,1,0:T(8,128)(2,1)S(1)}, u32[]{:S(2)}, u32[]{:S(2)}) collective-permute-start(bf16[1,4,64,1024]{3,2,1,0:T(8,128)(2,1)} %refs_0_.1), channel_id=1, source_target_pairs={{2,0},{4,2},{6,4},{0,6},{3,1},{5,3},{7,5},{1,7},{10,8},{12,10},{14... | collective-permute-start | bytes 1572872 | tf_op jit(solution)/shard_map/ppermute | solution.py:21
  3.2 13.6 %collective-permute-start = (bf16[1,4,64,1024]{3,2,1,0:T(8,128)(2,1)}, bf16[1,4,64,1024]{3,2,1,0:T(8,128)(2,1)}, u32[]{:S(2)}, u32[]{:S(2)}) collective-permute-start(bf16[1,4,64,1024]{3,2,1,0:T(8,128)(2,1)} %refs_0_.1), channel_id=1, source_target_pairs={{8,0},{0,8},{9,1},{1,9},{10,2},{2,10},{11,3},{3,11},{12,4},{4,12},... | collective-permute-start | bytes 1572872 | tf_op jit(solution)/shard_map/ppermute | solution.py:21
  15.1 115.2 %copy-start.8 = (bf16[1,4,64,1024]{3,2,1,0:T(8,128)(2,1)}, bf16[1,4,64,1024]{3,2,1,0:T(8,128)(2,1)S(1)}, u32[]{:S(2)}) copy-start(bf16[1,4,64,1024]{3,2,1,0:T(8,128)(2,1)S(1)} %collective-permute-done.2.refs_4_) | copy-start | bytes 1572868
  15.1 115.2 %copy-start.9 = (bf16[1,4,64,1024]{3,2,1,0:T(8,128)(2,1)}, bf16[1,4,64,1024]{3,2,1,0:T(8,128)(2,1)S(1)}, u32[]{:S(2)}) copy-start(bf16[1,4,64,1024]{3,2,1,0:T(8,128)(2,1)S(1)} %collective-permute-done.1.refs_2_) | copy-start | bytes 1572868
  17.7 14.1 %collective-permute-start.7 = (bf16[1,4,64,1024]{3,2,1,0:T(8,128)(2,1)}, bf16[1,4,64,1024]{3,2,1,0:T(8,128)(2,1)}, u32[]{:S(2)}, u32[]{:S(2)}) collective-permute-start(bf16[1,4,64,1024]{3,2,1,0:T(8,128)(2,1)} %broadcast_select_fusion.2), channel_id=1, source_target_pairs={{2,0},{7,1},{4,2},{1,3},{6,4},{3,5},{0,6},{5,7},{10,8},{15,9},{12,... | collective-permute-start | bytes 1572872 | tf_op jit(solution)/shard_map/ppermute | solution.py:31
  19.3 23.7 %collective-permute-start.4 = (bf16[1,1024,256]{2,1,0:T(8,128)(2,1)S(1)}, bf16[1,1024,256]{2,1,0:T(8,128)(2,1)}, u32[]{:S(2)}, u32[]{:S(2)}) collective-permute-start(bf16[1,1024,256]{2,1,0:T(8,128)(2,1)S(1)} %copy-done.1), channel_id=1, source_target_pairs={{48,0},{0,16},{16,32},{32,48},{49,1},{1,17},{17,33},{33,49},{50,2}... | collective-permute-start | bytes 1572872 | tf_op jit(solution)/shard_map/ppermute | solution.py:21
  23.5 23.7 %collective-permute-start.3 = (bf16[1,1024,256]{2,1,0:T(8,128)(2,1)S(1)}, bf16[1,1024,256]{2,1,0:T(8,128)(2,1)S(1)}, u32[]{:S(2)}, u32[]{:S(2)}) collective-permute-start(bf16[1,1024,256]{2,1,0:T(8,128)(2,1)S(1)} %copy-done.1), channel_id=1, source_target_pairs={{16,0},{32,16},{48,32},{0,48},{17,1},{33,17},{49,33},{1,49},{18,2}... | collective-permute-start | bytes 1572872 | tf_op jit(solution)/shard_map/ppermute | solution.py:21
  23.5 23.7 %collective-permute-start.6 = (bf16[1,4,64,1024]{3,2,1,0:T(8,128)(2,1)}, bf16[1,4,64,1024]{3,2,1,0:T(8,128)(2,1)S(1)}, u32[]{:S(2)}, u32[]{:S(2)}) collective-permute-start(bf16[1,4,64,1024]{3,2,1,0:T(8,128)(2,1)} %collective-permute-done.refs_1_), channel_id=1, source_target_pairs={{6,0},{0,2},{2,4},{4,6},{7,1},{1,3},{3,5},{5,7},{14,8},{8,10},{10,... | collective-permute-start | bytes 1572872 | tf_op jit(solution)/shard_map/ppermute | solution.py:21
  24.0 23.2 %collective-permute-start.5 = (bf16[1,4,64,1024]{3,2,1,0:T(8,128)(2,1)}, bf16[1,4,64,1024]{3,2,1,0:T(8,128)(2,1)S(1)}, u32[]{:S(2)}, u32[]{:S(2)}) collective-permute-start(bf16[1,4,64,1024]{3,2,1,0:T(8,128)(2,1)} %collective-permute-done.refs_1_), channel_id=1, source_target_pairs={{2,0},{4,2},{6,4},{0,6},{3,1},{5,3},{7,5},{1,7},{10,8},{12,10},{14... | collective-permute-start | bytes 1572872 | tf_op jit(solution)/shard_map/ppermute | solution.py:21
  48.2 60.8 %all-to-all-start.1 = ((bf16[16,64,2048]{2,1,0:T(8,128)(2,1)}), bf16[16,64,2048]{2,1,0:T(8,128)(2,1)}, u32[]{:S(2)}, u32[]{:S(2)}) async-start(bf16[16,64,2048]{2,1,0:T(8,128)(2,1)} %split_points.3), calls=%async_computation.1 | async-start | bytes 8388608 | tf_op jit(solution)/shard_map/all_to_all | solution.py:264
  56.5 44.3 %collective-permute-start.10 = (bf16[3,1024,256]{2,1,0:T(8,128)(2,1)}, bf16[3,1024,256]{2,1,0:T(8,128)(2,1)S(1)}, u32[]{:S(2)}, u32[]{:S(2)}) collective-permute-start(bf16[3,1024,256]{2,1,0:T(8,128)(2,1)} %get-tuple-element.49.refs_16_), channel_id=1, source_target_pairs={{192,0},{0,64},{64,128},{128,192},{193,1},{1,65},{65,129},{129,193... | collective-permute-start | bytes 4718600 | tf_op jit(solution)/shard_map/ppermute | solution.py:21
  57.8 43.1 %collective-permute-start.9 = (bf16[3,1024,256]{2,1,0:T(8,128)(2,1)}, bf16[3,1024,256]{2,1,0:T(8,128)(2,1)}, u32[]{:S(2)}, u32[]{:S(2)}) collective-permute-start(bf16[3,1024,256]{2,1,0:T(8,128)(2,1)} %get-tuple-element.49.refs_16_), channel_id=1, source_target_pairs={{64,0},{128,64},{192,128},{0,192},{65,1},{129,65},{193,129},{1,193... | collective-permute-start | bytes 4718600 | tf_op jit(solution)/shard_map/ppermute | solution.py:21
  59.4 41.4 %collective-permute-start.11 = (bf16[1,4,64,1024]{3,2,1,0:T(8,128)(2,1)}, bf16[1,4,64,1024]{3,2,1,0:T(8,128)(2,1)}, u32[]{:S(2)}, u32[]{:S(2)}) collective-permute-start(bf16[1,4,64,1024]{3,2,1,0:T(8,128)(2,1)} %broadcast_select_fusion.1), channel_id=1, source_target_pairs={{2,0},{7,1},{4,2},{1,3},{6,4},{3,5},{0,6},{5,7},{10,8},{15,9},{12,... | collective-permute-start | bytes 1572872 | tf_op jit(solution)/shard_map/ppermute | solution.py:31
  62.4 38.5 %collective-permute-start.8 = (bf16[1,1024,256]{2,1,0:T(8,128)(2,1)}, bf16[1,1024,256]{2,1,0:T(8,128)(2,1)}, u32[]{:S(2)}, u32[]{:S(2)}) collective-permute-start(bf16[1,1024,256]{2,1,0:T(8,128)(2,1)} %get-tuple-element.50), channel_id=1, source_target_pairs={{16,0},{49,1},{32,16},{1,17},{48,32},{17,33},{0,48},{33,49},{18,2}... | collective-permute-start | bytes 1572872 | tf_op jit(solution)/shard_map/ppermute | solution.py:31
  100.8 26.3 %copy-start.7 = (bf16[3,1024,256]{2,1,0:T(8,128)(2,1)}, bf16[3,1024,256]{2,1,0:T(8,128)(2,1)S(1)}, u32[]{:S(2)}) copy-start(bf16[3,1024,256]{2,1,0:T(8,128)(2,1)S(1)} %collective-permute-done.10.refs_19_) | copy-start | bytes 4718596
  109.0 72.0 %all-to-all-start = ((bf16[16,64,2048]{2,1,0:T(8,128)(2,1)}), bf16[16,64,2048]{2,1,0:T(8,128)(2,1)}, u32[]{:S(2)}, u32[]{:S(2)}) async-start(bf16[16,64,2048]{2,1,0:T(8,128)(2,1)} %split_points.2), calls=%async_computation | async-start | bytes 8388608 | tf_op jit(solution)/shard_map/all_to_all | solution.py:264
  124.8 5.6 %collective-permute-start.12 = (bf16[1,4,64,1024]{3,2,1,0:T(8,128)(2,1)}, bf16[1,4,64,1024]{3,2,1,0:T(8,128)(2,1)S(1)}, u32[]{:S(2)}, u32[]{:S(2)}) collective-permute-start(bf16[1,4,64,1024]{3,2,1,0:T(8,128)(2,1)} %refs_0_.1), channel_id=1, source_target_pairs={{0,1},{1,0},{2,3},{3,2},{4,5},{5,4},{6,7},{7,6},{8,9},{9,8},{10,11... | collective-permute-start | bytes 1572872 | tf_op jit(solution)/shard_map/ppermute | solution.py:16
  125.1 15.0 %collective-permute-start.22 = (bf16[1,1024,256]{2,1,0:T(8,128)(2,1)}, bf16[1,1024,256]{2,1,0:T(8,128)(2,1)S(1)}, u32[]{:S(2)}, u32[]{:S(2)}) collective-permute-start(bf16[1,1024,256]{2,1,0:T(8,128)(2,1)} %collective-permute-done.8.refs_20_), channel_id=1, source_target_pairs={{192,0},{0,64},{64,128},{128,192},{193,1},{1,65},{65,129},{129,193... | collective-permute-start | bytes 1572872 | tf_op jit(solution)/shard_map/ppermute | solution.py:21
  126.4 14.0 %collective-permute-start.21 = (bf16[1,1024,256]{2,1,0:T(8,128)(2,1)}, bf16[1,1024,256]{2,1,0:T(8,128)(2,1)S(1)}, u32[]{:S(2)}, u32[]{:S(2)}) collective-permute-start(bf16[1,1024,256]{2,1,0:T(8,128)(2,1)} %collective-permute-done.8.refs_20_), channel_id=1, source_target_pairs={{64,0},{128,64},{192,128},{0,192},{65,1},{129,65},{193,129},{1,193... | collective-permute-start | bytes 1572872 | tf_op jit(solution)/shard_map/ppermute | solution.py:21
  129.9 33.1 %collective-permute-start.20 = (bf16[3,1024,256]{2,1,0:T(8,128)(2,1)}, bf16[3,1024,256]{2,1,0:T(8,128)(2,1)}, u32[]{:S(2)}, u32[]{:S(2)}) collective-permute-start(bf16[3,1024,256]{2,1,0:T(8,128)(2,1)} %broadcast_select_fusion), channel_id=1, source_target_pairs={{64,0},{193,1},{128,64},{1,65},{192,128},{65,129},{0,192},{129,193... | collective-permute-start | bytes 4718600 | tf_op jit(solution)/shard_map/ppermute | solution.py:31
  130.3 11.2 %collective-permute-start.14 = (bf16[1,4,64,1024]{3,2,1,0:T(8,128)(2,1)S(1)}, bf16[1,4,64,1024]{3,2,1,0:T(8,128)(2,1)S(1)}, u32[]{:S(2)}, u32[]{:S(2)}) collective-permute-start(bf16[1,4,64,1024]{3,2,1,0:T(8,128)(2,1)S(1)} %collective-permute-done.1.refs_2_), channel_id=1, source_target_pairs={{0,1},{1,0},{2,3},{3,2},{4,5},{5,4},{6,7},{7,6},{8,9},{9,8},{10,11... | collective-permute-start | bytes 1572872 | tf_op jit(solution)/shard_map/ppermute | solution.py:16
  130.3 11.5 %collective-permute-start.16 = (bf16[1,4,64,1024]{3,2,1,0:T(8,128)(2,1)S(1)}, bf16[1,4,64,1024]{3,2,1,0:T(8,128)(2,1)S(1)}, u32[]{:S(2)}, u32[]{:S(2)}) collective-permute-start(bf16[1,4,64,1024]{3,2,1,0:T(8,128)(2,1)S(1)} %collective-permute-done.2.refs_4_), channel_id=1, source_target_pairs={{0,1},{1,0},{2,3},{3,2},{4,5},{5,4},{6,7},{7,6},{8,9},{9,8},{10,11... | collective-permute-start | bytes 1572872 | tf_op jit(solution)/shard_map/ppermute | solution.py:16
  140.1 2.1 collective-permute-start.13
  140.4 2.6 %collective-permute-start.18 = (bf16[1,4,64,1024]{3,2,1,0:T(8,128)(2,1)}, bf16[1,4,64,1024]{3,2,1,0:T(8,128)(2,1)S(1)}, u32[]{:S(2)}, u32[]{:S(2)}) collective-permute-start(bf16[1,4,64,1024]{3,2,1,0:T(8,128)(2,1)} %collective-permute-done.7.refs_6_), channel_id=1, source_target_pairs={{0,1},{1,0},{2,3},{3,2},{4,5},{5,4},{6,7},{7,6},{8,9},{9,8},{10,11... | collective-permute-start | bytes 1572872 | tf_op jit(solution)/shard_map/ppermute | solution.py:16
  141.5 3.6 %collective-permute-start.15 = (bf16[1,4,64,1024]{3,2,1,0:T(8,128)(2,1)S(1)}, bf16[1,4,64,1024]{3,2,1,0:T(8,128)(2,1)S(1)}, u32[]{:S(2)}, u32[]{:S(2)}) collective-permute-start(bf16[1,4,64,1024]{3,2,1,0:T(8,128)(2,1)S(1)} %copy-done.15), channel_id=1, source_target_pairs={{0,1},{1,0},{2,3},{3,2},{4,5},{5,4},{6,7},{7,6},{8,9},{9,8},{10,11... | collective-permute-start | bytes 1572872 | tf_op jit(solution)/shard_map/ppermute | solution.py:16
  141.9 3.2 %collective-permute-start.17 = (bf16[1,4,64,1024]{3,2,1,0:T(8,128)(2,1)S(1)}, bf16[1,4,64,1024]{3,2,1,0:T(8,128)(2,1)S(1)}, u32[]{:S(2)}, u32[]{:S(2)}) collective-permute-start(bf16[1,4,64,1024]{3,2,1,0:T(8,128)(2,1)S(1)} %copy-done.12), channel_id=1, source_target_pairs={{0,1},{1,0},{2,3},{3,2},{4,5},{5,4},{6,7},{7,6},{8,9},{9,8},{10,11... | collective-permute-start | bytes 1572872 | tf_op jit(solution)/shard_map/ppermute | solution.py:16
  142.2 3.1 %collective-permute-start.19 = (bf16[1,4,64,1024]{3,2,1,0:T(8,128)(2,1)}, bf16[1,4,64,1024]{3,2,1,0:T(8,128)(2,1)}, u32[]{:S(2)}, u32[]{:S(2)}) collective-permute-start(bf16[1,4,64,1024]{3,2,1,0:T(8,128)(2,1)} %collective-permute-done.11.refs_7_), channel_id=1, source_target_pairs={{0,1},{1,0},{2,3},{3,2},{4,5},{5,4},{6,7},{7,6},{8,9},{9,8},{10,11... | collective-permute-start | bytes 1572872 | tf_op jit(solution)/shard_map/ppermute | solution.py:16
  143.8 19.2 %collective-permute-start.23 = (bf16[1,1024,256]{2,1,0:T(8,128)(2,1)}, bf16[1,1024,256]{2,1,0:T(8,128)(2,1)}, u32[]{:S(2)}, u32[]{:S(2)}) collective-permute-start(bf16[1,1024,256]{2,1,0:T(8,128)(2,1)} %broadcast_select_fusion.3), channel_id=1, source_target_pairs={{64,0},{193,1},{128,64},{1,65},{192,128},{65,129},{0,192},{129,193... | collective-permute-start | bytes 1572872 | tf_op jit(solution)/shard_map/ppermute | solution.py:31
  145.1 28.6 %copy-start.4 = (f32[1,2048]{1,0:T(1,128)S(1)}, f32[1,2048]{1,0:T(1,128)}, u32[]{:S(2)}) copy-start(f32[1,2048]{1,0:T(1,128)} %p_ref.1) | copy-start | bytes 24580
  187.8 3.1 %collective-permute-start.24 = (f32[8,10,16,256]{3,2,1,0:T(8,128)S(1)}, f32[8,10,16,256]{3,2,1,0:T(8,128)S(1)}, u32[]{:S(2)}, u32[]{:S(2)}) collective-permute-start(f32[8,10,16,256]{3,2,1,0:T(8,128)S(1)} %get-tuple-element.47), channel_id=1, source_target_pairs={{0,1},{1,0},{2,3},{3,2},{4,5},{5,4},{6,7},{7,6},{8,9},{9,8},{10,11... | collective-permute-start | bytes 3932168 | tf_op jit(solution)/shard_map/ppermute | solution.py:16
  235.1 2.1 collective-permute-start.25
  (22 other events, 189.0 us)

commit v3 on v2

--- a/solution.py
+++ b/solution.py
@@ -296,8 +296,9 @@
     derivs, hopped, part = barrier((derivs, hopped, part))
 
     keep, send = deriv_part(pos, derivs.reshape(width, -1), part)
-    part = keep + swap_cores(send)
-    part = lax.all_to_all(part, CHIPS, 0, 0, tiled=True).sum(0).astype(jnp.bfloat16)
+    part = (keep + swap_cores(send)).astype(jnp.bfloat16)
+    part = lax.all_to_all(part, CHIPS, 0, 0, tiled=True).astype(jnp.float32)
+    part = part.sum(0).astype(jnp.bfloat16)
     chips = lax.axis_size(CHIPS)
     low = jnp.broadcast_to(part[None], (chips, *part.shape))
     low = lax.all_to_all(low, CHIPS, 0, 0, tiled=True)

time: 243 us -> 236 us (0.971)
  blocking collectives: 43.7 us -> 36.6 us
    all_to_all x1, blocking collectives: 29.4 us -> 22.5 us  [local(): part = lax.all_to_all(part, CHIPS, 0, 0, tiled=True).astype(jnp.float32)]
  transfers between devices with their start and end apart: 28 -> 28, of which waited for: 15 -> 15; matrix products, arithmetic and copies ran while one was open for 4% -> 4% of each run, Pallas kernels for 10% -> 11%
where the time goes in v3:
time: 236 us; the launch traced here: 232 us
  waiting for transfers between devices  103 us (44%)
  starting transfers between devices  44.9 us (19%)
  blocking collectives  36.6 us (16%)
  Pallas kernels  31.9 us (14%)
  local copies, waits for them, and re-layouts  8.11 us (3%)
  other arithmetic  7.81 us (3%)
    ppermute x5, waiting for transfers between devices, far(): return lax.ppermute(held, (axis, 'c'), pairs)  51.8 us
    ppermute x11, waiting for transfers between devices, shift(): return lax.ppermute(a, axis, [((i + step) % size, i) for i in range(size)])  36.6 us
    all_to_all x1, blocking collectives, local(): part = lax.all_to_all(part, CHIPS, 0, 0, tiled=True).astype(jnp.float32)  22.5 us
    all_to_all x2, starting transfers between devices, exchange(): return lax.all_to_all(a, GRP, 0, 0, tiled=True)  20.3 us
    ppermute x11, starting transfers between devices, shift(): return lax.ppermute(a, axis, [((i + step) % size, i) for i in range(size)])  16.7 us
    all_to_all x1, blocking collectives, local(): low = lax.all_to_all(low, CHIPS, 0, 0, tiled=True)  14.1 us
    pallas_call x1, Pallas kernels, hop_apply(): pl.pallas_call(hop_kernel, out_shape=jax.ShapeDtypeStruct((blocks * rows,...  10.7 us
    all_to_all x2, waiting for transfers between devices, exchange(): return lax.all_to_all(a, GRP, 0, 0, tiled=True)  8.77 us
  transfers between devices with their start and end apart: 28, of which 15 were waited for; matrix products, arithmetic and copies ran while one was open for 4% of the time, Pallas kernels for 11%

profile of v3, /device:TPU:80, one launch (start us, length us, event | category | flops | bytes accessed | tf_op | source)
XLA Modules:
  0.0 232.5 jit_solution(17923203493691853768)
XLA Ops:
  0.0 1.5 collective-permute-start.2
  1.5 1.7 collective-permute-start.1
  3.2 1.9 collective-permute-start
  5.2 9.9 %collective-permute-done.2.refs_4_ = bf16[1,4,64,1024]{3,2,1,0:T(8,128)(2,1)S(1)} collective-permute-done((bf16[1,4,64,1024]{3,2,1,0:T(8,128)(2,1)}, bf16[1,4,64,1024]{3,2,1,0:T(8,128)(2,1)S(1)}, u32[]{:S(2)}, u32[]{:S(2)}) %collective-permute-start.2) | collective-permute-done | bytes 524320 | tf_op jit(solution)/shard_map/ppermute | solution.py:21
  15.1 1.8 collective-permute-done.refs_1_
  17.7 1.5 collective-permute-start.7
  19.3 4.3 %collective-permute-start.4 = (bf16[1,1024,256]{2,1,0:T(8,128)(2,1)S(1)}, bf16[1,1024,256]{2,1,0:T(8,128)(2,1)}, u32[]{:S(2)}, u32[]{:S(2)}) collective-permute-start(bf16[1,1024,256]{2,1,0:T(8,128)(2,1)S(1)} %copy-done.1), channel_id=1, source_target_pairs={{48,0},{0,16},{16,32},{32,48},{49,1},{1,17},{17,33},{33,49},{50,2}... | collective-permute-start | bytes 1572872 | tf_op jit(solution)/shard_map/ppermute | solution.py:21
  24.0 2.8 %collective-permute-start.5 = (bf16[1,4,64,1024]{3,2,1,0:T(8,128)(2,1)}, bf16[1,4,64,1024]{3,2,1,0:T(8,128)(2,1)S(1)}, u32[]{:S(2)}, u32[]{:S(2)}) collective-permute-start(bf16[1,4,64,1024]{3,2,1,0:T(8,128)(2,1)} %collective-permute-done.refs_1_), channel_id=1, source_target_pairs={{2,0},{4,2},{6,4},{0,6},{3,1},{5,3},{7,5},{1,7},{10,8},{12,10},{14... | collective-permute-start | bytes 1572872 | tf_op jit(solution)/shard_map/ppermute | solution.py:21
  27.4 4.3 %split_points.3 = bf16[16,64,2048]{2,1,0:T(8,128)(2,1)} custom-call(bf16[64,32768]{1,0:T(8,128)(2,1)} %bitcast.11), custom_call_target="tpu_custom_call" | custom-call | bytes 8388608 | tf_op jit(solution)/shard_map/split_points/pallas_call | solution.py:49
  31.8 11.2 %collective-permute-done.4 = bf16[1,1024,256]{2,1,0:T(8,128)(2,1)} collective-permute-done((bf16[1,1024,256]{2,1,0:T(8,128)(2,1)S(1)}, bf16[1,1024,256]{2,1,0:T(8,128)(2,1)}, u32[]{:S(2)}, u32[]{:S(2)}) %collective-permute-start.4) | collective-permute-done | bytes 524320 | tf_op jit(solution)/shard_map/ppermute | solution.py:21
  43.0 4.2 %collective-permute-done.3 = bf16[1,1024,256]{2,1,0:T(8,128)(2,1)S(1)} collective-permute-done((bf16[1,1024,256]{2,1,0:T(8,128)(2,1)S(1)}, bf16[1,1024,256]{2,1,0:T(8,128)(2,1)S(1)}, u32[]{:S(2)}, u32[]{:S(2)}) %collective-permute-start.3) | collective-permute-done | bytes 524320 | tf_op jit(solution)/shard_map/ppermute | solution.py:21
  48.2 4.5 %all-to-all-start.1 = ((bf16[16,64,2048]{2,1,0:T(8,128)(2,1)}), bf16[16,64,2048]{2,1,0:T(8,128)(2,1)}, u32[]{:S(2)}, u32[]{:S(2)}) async-start(bf16[16,64,2048]{2,1,0:T(8,128)(2,1)} %split_points.3), calls=%async_computation.1 | async-start | bytes 8388608 | tf_op jit(solution)/shard_map/all_to_all | solution.py:264
  54.4 2.1 constant_dynamic-update-slice_fusion
  56.5 1.3 collective-permute-start.10
  59.4 3.0 %collective-permute-start.11 = (bf16[1,4,64,1024]{3,2,1,0:T(8,128)(2,1)}, bf16[1,4,64,1024]{3,2,1,0:T(8,128)(2,1)}, u32[]{:S(2)}, u32[]{:S(2)}) collective-permute-start(bf16[1,4,64,1024]{3,2,1,0:T(8,128)(2,1)} %broadcast_select_fusion.1), channel_id=1, source_target_pairs={{2,0},{7,1},{4,2},{1,3},{6,4},{3,5},{0,6},{5,7},{10,8},{15,9},{12,... | collective-permute-start | bytes 1572872 | tf_op jit(solution)/shard_map/ppermute | solution.py:31
  62.4 4.3 %split_points.2 = bf16[16,64,2048]{2,1,0:T(8,128)(2,1)} custom-call(bf16[64,32768]{1,0:T(8,128)(2,1)} %bitcast.12), custom_call_target="tpu_custom_call" | custom-call | bytes 8388608 | tf_op jit(solution)/shard_map/split_points/pallas_call | solution.py:49
  66.7 34.2 %collective-permute-done.11.refs_7_ = bf16[1,4,64,1024]{3,2,1,0:T(8,128)(2,1)} collective-permute-done((bf16[1,4,64,1024]{3,2,1,0:T(8,128)(2,1)}, bf16[1,4,64,1024]{3,2,1,0:T(8,128)(2,1)}, u32[]{:S(2)}, u32[]{:S(2)}) %collective-permute-start.11) | collective-permute-done | bytes 524320 | tf_op jit(solution)/shard_map/ppermute | solution.py:31
  100.9 8.1 %all-to-all-done.1 = bf16[16,64,2048]{2,1,0:T(8,128)(2,1)} async-done(((bf16[16,64,2048]{2,1,0:T(8,128)(2,1)}), bf16[16,64,2048]{2,1,0:T(8,128)(2,1)}, u32[]{:S(2)}, u32[]{:S(2)}) %all-to-all-start.1) | async-done | bytes 4194336 | tf_op jit(solution)/shard_map/all_to_all | solution.py:264
  109.0 15.8 %all-to-all-start = ((bf16[16,64,2048]{2,1,0:T(8,128)(2,1)}), bf16[16,64,2048]{2,1,0:T(8,128)(2,1)}, u32[]{:S(2)}, u32[]{:S(2)}) async-start(bf16[16,64,2048]{2,1,0:T(8,128)(2,1)} %split_points.2), calls=%async_computation | async-start | bytes 8388608 | tf_op jit(solution)/shard_map/all_to_all | solution.py:264
  127.1 2.7 %broadcast_select_fusion = bf16[3,1024,256]{2,1,0:T(8,128)(2,1)} fusion(bf16[3,1024,256]{2,1,0:T(8,128)(2,1)} %collective-permute-done.9.refs_17_, bf16[3,1024,256]{2,1,0:T(8,128)(2,1)S(1)} %collective-permute-done.10.refs_19_, pred[]{:T(512)S(6)} %eq.2), kind=kLoop, calls=%fused_computation | loop fusion | flops 786432 | bytes 4718593 | tf_op jit(solution)/shard_map/jit(_where)/select_n | solution.py:26
  130.9 9.2 %collective-permute-done.22.refs_23_ = bf16[1,1024,256]{2,1,0:T(8,128)(2,1)S(1)} collective-permute-done((bf16[1,1024,256]{2,1,0:T(8,128)(2,1)}, bf16[1,1024,256]{2,1,0:T(8,128)(2,1)S(1)}, u32[]{:S(2)}, u32[]{:S(2)}) %collective-permute-start.22) | collective-permute-done | bytes 524320 | tf_op jit(solution)/shard_map/ppermute | solution.py:21
  145.3 17.6 %collective-permute-done.23.refs_22_ = bf16[1,1024,256]{2,1,0:T(8,128)(2,1)} collective-permute-done((bf16[1,1024,256]{2,1,0:T(8,128)(2,1)}, bf16[1,1024,256]{2,1,0:T(8,128)(2,1)}, u32[]{:S(2)}, u32[]{:S(2)}) %collective-permute-start.23) | collective-permute-done | bytes 524320 | tf_op jit(solution)/shard_map/ppermute | solution.py:31
  163.0 10.7 %hop_apply.1.h_ref = f32[1024,256]{1,0:T(8,128)} custom-call(s32[6]{0:T(128)} %stack.27.pos, s32[16]{0:T(128)} %counts.3, s32[16,4]{1,0:T(8,128)} %copy.8.near, bf16[1,4,64,1024]{3,2,1,0:T(8,128)(2,1)} %refs_0_.1, bf16[1,4,64,1024]{3,2,1,0:T(8,128)(2,1)} %collective-permute-done.refs_1_, bf16[1,4,64,1024]{3,2,1,0:T(8,128)(2,1)} %copy-done.9, ...), custom_call_target="tpu_custom_call" | custom-call | flops 2147483648 | bytes 10485760 | tf_op jit(solution)/shard_map/hop_apply/pallas_call | solution.py:193
  173.7 5.1 %value_part.1.g_ref = f32[10,256,256]{2,1,0:T(8,128)S(1)} custom-call(f32[1,2048]{1,0:T(1,128)S(1)} %copy-done.4, bf16[1024,2048]{1,0:T(8,128)(2,1)} %bitcast.8.v_ref), custom_call_target="tpu_custom_call" | custom-call | flops 2684354560 | bytes 6815744 | tf_op jit(solution)/shard_map/value_part/pallas_call | solution.py:82
  178.8 1.5 copy-done.5
  181.0 1.7 copy-done.6
  182.7 5.1 %deriv_part.1 = (f32[8,10,16,256]{3,2,1,0:T(8,128)S(1)}, f32[8,10,16,256]{3,2,1,0:T(8,128)S(1)}) custom-call(s32[6]{0:T(128)S(1)} %copy-done.2, bf16[1024,2048]{1,0:T(8,128)(2,1)} %bitcast.9.d_ref, f32[10,256,256]{2,1,0:T(8,128)S(1)} %copy-done.6), custom_call_target="tpu_custom_call" | custom-call | flops 2684354560 | bytes 9437184 | tf_op jit(solution)/shard_map/deriv_part/pallas_call | solution.py:123
  187.9 3.0 %collective-permute-done.24 = f32[8,10,16,256]{3,2,1,0:T(8,128)S(1)} collective-permute-done((f32[8,10,16,256]{3,2,1,0:T(8,128)S(1)}, f32[8,10,16,256]{3,2,1,0:T(8,128)S(1)}, u32[]{:S(2)}, u32[]{:S(2)}) %collective-permute-start.24) | collective-permute-done | bytes 1310752 | tf_op jit(solution)/shard_map/ppermute | solution.py:16
  191.3 22.5 %all_to_all.20 = bf16[8,10,16,256]{3,2,1,0:T(8,128)(2,1)S(1)} all-to-all(bf16[8,10,16,256]{3,2,1,0:T(8,128)(2,1)S(1)} %add_convert_fusion), channel_id=1, replica_groups=mesh['y'=4,'zh'=4,'zl'=2,'x'=4,'c'=2] {'zl','x'}, dimensions={0} | all-to-all | bytes 1310720 | tf_op jit(solution)/shard_map/all_to_all | solution.py:300
  213.9 14.1 %all_to_all.21.mine_ref = bf16[8,10,16,256]{3,2,1,0:T(8,128)(2,1)S(1)} all-to-all(bf16[8,10,16,256]{3,2,1,0:T(8,128)(2,1)S(1)} %broadcast_in_dim.4), channel_id=1, replica_groups=mesh['y'=4,'zh'=4,'zl'=2,'x'=4,'c'=2] {'zl','x'}, dimensions={0} | all-to-all | bytes 1310720 | tf_op jit(solution)/shard_map/all_to_all | solution.py:304
  228.0 2.1 collective-permute-done.25.other_ref
  230.1 2.3 %own_apply.1 = f32[1024,256]{1,0:T(8,128)} custom-call(s32[6]{0:T(128)S(1)} %copy-done.2, s32[16]{0:T(128)S(1)} %copy-done.3, bf16[8,10,16,256]{3,2,1,0:T(8,128)(2,1)S(1)} %all_to_all.21.mine_ref, bf16[8,10,16,256]{3,2,1,0:T(8,128)(2,1)S(1)} %collective-permute-done.25.other_ref, bf16[1,1024,256]{2,1,0:T(8,128)(2,1)S(1)} %copy-done.1, f32[1024,256]{1,0:T(8,128)S(1)} %copy-done), custom_call_target="tpu_custom_call" | custom-call | flops 536870912 | bytes 3932160 | tf_op jit(solution)/shard_map/own_apply/pallas_call | solution.py:243
  (96 shorter events, 16.1 us)
Async XLA Ops:
  0.0 15.1 %collective-permute-start.2 = (bf16[1,4,64,1024]{3,2,1,0:T(8,128)(2,1)}, bf16[1,4,64,1024]{3,2,1,0:T(8,128)(2,1)S(1)}, u32[]{:S(2)}, u32[]{:S(2)}) collective-permute-start(bf16[1,4,64,1024]{3,2,1,0:T(8,128)(2,1)} %refs_0_.1), channel_id=1, source_target_pairs={{6,0},{0,2},{2,4},{4,6},{7,1},{1,3},{3,5},{5,7},{14,8},{8,10},{10,... | collective-permute-start | bytes 1572872 | tf_op jit(solution)/shard_map/ppermute | solution.py:21
  1.5 13.6 %collective-permute-start.1 = (bf16[1,4,64,1024]{3,2,1,0:T(8,128)(2,1)}, bf16[1,4,64,1024]{3,2,1,0:T(8,128)(2,1)S(1)}, u32[]{:S(2)}, u32[]{:S(2)}) collective-permute-start(bf16[1,4,64,1024]{3,2,1,0:T(8,128)(2,1)} %refs_0_.1), channel_id=1, source_target_pairs={{2,0},{4,2},{6,4},{0,6},{3,1},{5,3},{7,5},{1,7},{10,8},{12,10},{14... | collective-permute-start | bytes 1572872 | tf_op jit(solution)/shard_map/ppermute | solution.py:21
  3.2 13.6 %collective-permute-start = (bf16[1,4,64,1024]{3,2,1,0:T(8,128)(2,1)}, bf16[1,4,64,1024]{3,2,1,0:T(8,128)(2,1)}, u32[]{:S(2)}, u32[]{:S(2)}) collective-permute-start(bf16[1,4,64,1024]{3,2,1,0:T(8,128)(2,1)} %refs_0_.1), channel_id=1, source_target_pairs={{8,0},{0,8},{9,1},{1,9},{10,2},{2,10},{11,3},{3,11},{12,4},{4,12},... | collective-permute-start | bytes 1572872 | tf_op jit(solution)/shard_map/ppermute | solution.py:21
  15.1 115.2 %copy-start.8 = (bf16[1,4,64,1024]{3,2,1,0:T(8,128)(2,1)}, bf16[1,4,64,1024]{3,2,1,0:T(8,128)(2,1)S(1)}, u32[]{:S(2)}) copy-start(bf16[1,4,64,1024]{3,2,1,0:T(8,128)(2,1)S(1)} %collective-permute-done.2.refs_4_) | copy-start | bytes 1572868
  15.1 115.2 %copy-start.9 = (bf16[1,4,64,1024]{3,2,1,0:T(8,128)(2,1)}, bf16[1,4,64,1024]{3,2,1,0:T(8,128)(2,1)S(1)}, u32[]{:S(2)}) copy-start(bf16[1,4,64,1024]{3,2,1,0:T(8,128)(2,1)S(1)} %collective-permute-done.1.refs_2_) | copy-start | bytes 1572868
  17.7 14.1 %collective-permute-start.7 = (bf16[1,4,64,1024]{3,2,1,0:T(8,128)(2,1)}, bf16[1,4,64,1024]{3,2,1,0:T(8,128)(2,1)}, u32[]{:S(2)}, u32[]{:S(2)}) collective-permute-start(bf16[1,4,64,1024]{3,2,1,0:T(8,128)(2,1)} %broadcast_select_fusion.2), channel_id=1, source_target_pairs={{2,0},{7,1},{4,2},{1,3},{6,4},{3,5},{0,6},{5,7},{10,8},{15,9},{12,... | collective-permute-start | bytes 1572872 | tf_op jit(solution)/shard_map/ppermute | solution.py:31
  19.3 23.7 %collective-permute-start.4 = (bf16[1,1024,256]{2,1,0:T(8,128)(2,1)S(1)}, bf16[1,1024,256]{2,1,0:T(8,128)(2,1)}, u32[]{:S(2)}, u32[]{:S(2)}) collective-permute-start(bf16[1,1024,256]{2,1,0:T(8,128)(2,1)S(1)} %copy-done.1), channel_id=1, source_target_pairs={{48,0},{0,16},{16,32},{32,48},{49,1},{1,17},{17,33},{33,49},{50,2}... | collective-permute-start | bytes 1572872 | tf_op jit(solution)/shard_map/ppermute | solution.py:21
  23.5 23.7 %collective-permute-start.3 = (bf16[1,1024,256]{2,1,0:T(8,128)(2,1)S(1)}, bf16[1,1024,256]{2,1,0:T(8,128)(2,1)S(1)}, u32[]{:S(2)}, u32[]{:S(2)}) collective-permute-start(bf16[1,1024,256]{2,1,0:T(8,128)(2,1)S(1)} %copy-done.1), channel_id=1, source_target_pairs={{16,0},{32,16},{48,32},{0,48},{17,1},{33,17},{49,33},{1,49},{18,2}... | collective-permute-start | bytes 1572872 | tf_op jit(solution)/shard_map/ppermute | solution.py:21
  23.5 23.7 %collective-permute-start.6 = (bf16[1,4,64,1024]{3,2,1,0:T(8,128)(2,1)}, bf16[1,4,64,1024]{3,2,1,0:T(8,128)(2,1)S(1)}, u32[]{:S(2)}, u32[]{:S(2)}) collective-permute-start(bf16[1,4,64,1024]{3,2,1,0:T(8,128)(2,1)} %collective-permute-done.refs_1_), channel_id=1, source_target_pairs={{6,0},{0,2},{2,4},{4,6},{7,1},{1,3},{3,5},{5,7},{14,8},{8,10},{10,... | collective-permute-start | bytes 1572872 | tf_op jit(solution)/shard_map/ppermute | solution.py:21
  24.0 23.2 %collective-permute-start.5 = (bf16[1,4,64,1024]{3,2,1,0:T(8,128)(2,1)}, bf16[1,4,64,1024]{3,2,1,0:T(8,128)(2,1)S(1)}, u32[]{:S(2)}, u32[]{:S(2)}) collective-permute-start(bf16[1,4,64,1024]{3,2,1,0:T(8,128)(2,1)} %collective-permute-done.refs_1_), channel_id=1, source_target_pairs={{2,0},{4,2},{6,4},{0,6},{3,1},{5,3},{7,5},{1,7},{10,8},{12,10},{14... | collective-permute-start | bytes 1572872 | tf_op jit(solution)/shard_map/ppermute | solution.py:21
  48.2 60.8 %all-to-all-start.1 = ((bf16[16,64,2048]{2,1,0:T(8,128)(2,1)}), bf16[16,64,2048]{2,1,0:T(8,128)(2,1)}, u32[]{:S(2)}, u32[]{:S(2)}) async-start(bf16[16,64,2048]{2,1,0:T(8,128)(2,1)} %split_points.3), calls=%async_computation.1 | async-start | bytes 8388608 | tf_op jit(solution)/shard_map/all_to_all | solution.py:264
  56.5 44.3 %collective-permute-start.10 = (bf16[3,1024,256]{2,1,0:T(8,128)(2,1)}, bf16[3,1024,256]{2,1,0:T(8,128)(2,1)S(1)}, u32[]{:S(2)}, u32[]{:S(2)}) collective-permute-start(bf16[3,1024,256]{2,1,0:T(8,128)(2,1)} %get-tuple-element.49.refs_16_), channel_id=1, source_target_pairs={{192,0},{0,64},{64,128},{128,192},{193,1},{1,65},{65,129},{129,193... | collective-permute-start | bytes 4718600 | tf_op jit(solution)/shard_map/ppermute | solution.py:21
  57.8 43.1 %collective-permute-start.9 = (bf16[3,1024,256]{2,1,0:T(8,128)(2,1)}, bf16[3,1024,256]{2,1,0:T(8,128)(2,1)}, u32[]{:S(2)}, u32[]{:S(2)}) collective-permute-start(bf16[3,1024,256]{2,1,0:T(8,128)(2,1)} %get-tuple-element.49.refs_16_), channel_id=1, source_target_pairs={{64,0},{128,64},{192,128},{0,192},{65,1},{129,65},{193,129},{1,193... | collective-permute-start | bytes 4718600 | tf_op jit(solution)/shard_map/ppermute | solution.py:21
  59.4 41.4 %collective-permute-start.11 = (bf16[1,4,64,1024]{3,2,1,0:T(8,128)(2,1)}, bf16[1,4,64,1024]{3,2,1,0:T(8,128)(2,1)}, u32[]{:S(2)}, u32[]{:S(2)}) collective-permute-start(bf16[1,4,64,1024]{3,2,1,0:T(8,128)(2,1)} %broadcast_select_fusion.1), channel_id=1, source_target_pairs={{2,0},{7,1},{4,2},{1,3},{6,4},{3,5},{0,6},{5,7},{10,8},{15,9},{12,... | collective-permute-start | bytes 1572872 | tf_op jit(solution)/shard_map/ppermute | solution.py:31
  62.4 38.5 %collective-permute-start.8 = (bf16[1,1024,256]{2,1,0:T(8,128)(2,1)}, bf16[1,1024,256]{2,1,0:T(8,128)(2,1)}, u32[]{:S(2)}, u32[]{:S(2)}) collective-permute-start(bf16[1,1024,256]{2,1,0:T(8,128)(2,1)} %get-tuple-element.50), channel_id=1, source_target_pairs={{16,0},{49,1},{32,16},{1,17},{48,32},{17,33},{0,48},{33,49},{18,2}... | collective-permute-start | bytes 1572872 | tf_op jit(solution)/shard_map/ppermute | solution.py:31
  100.8 26.3 %copy-start.7 = (bf16[3,1024,256]{2,1,0:T(8,128)(2,1)}, bf16[3,1024,256]{2,1,0:T(8,128)(2,1)S(1)}, u32[]{:S(2)}) copy-start(bf16[3,1024,256]{2,1,0:T(8,128)(2,1)S(1)} %collective-permute-done.10.refs_19_) | copy-start | bytes 4718596
  109.0 72.0 %all-to-all-start = ((bf16[16,64,2048]{2,1,0:T(8,128)(2,1)}), bf16[16,64,2048]{2,1,0:T(8,128)(2,1)}, u32[]{:S(2)}, u32[]{:S(2)}) async-start(bf16[16,64,2048]{2,1,0:T(8,128)(2,1)} %split_points.2), calls=%async_computation | async-start | bytes 8388608 | tf_op jit(solution)/shard_map/all_to_all | solution.py:264
  124.8 5.6 %collective-permute-start.12 = (bf16[1,4,64,1024]{3,2,1,0:T(8,128)(2,1)}, bf16[1,4,64,1024]{3,2,1,0:T(8,128)(2,1)S(1)}, u32[]{:S(2)}, u32[]{:S(2)}) collective-permute-start(bf16[1,4,64,1024]{3,2,1,0:T(8,128)(2,1)} %refs_0_.1), channel_id=1, source_target_pairs={{0,1},{1,0},{2,3},{3,2},{4,5},{5,4},{6,7},{7,6},{8,9},{9,8},{10,11... | collective-permute-start | bytes 1572872 | tf_op jit(solution)/shard_map/ppermute | solution.py:16
  125.1 15.0 %collective-permute-start.22 = (bf16[1,1024,256]{2,1,0:T(8,128)(2,1)}, bf16[1,1024,256]{2,1,0:T(8,128)(2,1)S(1)}, u32[]{:S(2)}, u32[]{:S(2)}) collective-permute-start(bf16[1,1024,256]{2,1,0:T(8,128)(2,1)} %collective-permute-done.8.refs_20_), channel_id=1, source_target_pairs={{192,0},{0,64},{64,128},{128,192},{193,1},{1,65},{65,129},{129,193... | collective-permute-start | bytes 1572872 | tf_op jit(solution)/shard_map/ppermute | solution.py:21
  126.4 14.0 %collective-permute-start.21 = (bf16[1,1024,256]{2,1,0:T(8,128)(2,1)}, bf16[1,1024,256]{2,1,0:T(8,128)(2,1)S(1)}, u32[]{:S(2)}, u32[]{:S(2)}) collective-permute-start(bf16[1,1024,256]{2,1,0:T(8,128)(2,1)} %collective-permute-done.8.refs_20_), channel_id=1, source_target_pairs={{64,0},{128,64},{192,128},{0,192},{65,1},{129,65},{193,129},{1,193... | collective-permute-start | bytes 1572872 | tf_op jit(solution)/shard_map/ppermute | solution.py:21
  129.9 33.1 %collective-permute-start.20 = (bf16[3,1024,256]{2,1,0:T(8,128)(2,1)}, bf16[3,1024,256]{2,1,0:T(8,128)(2,1)}, u32[]{:S(2)}, u32[]{:S(2)}) collective-permute-start(bf16[3,1024,256]{2,1,0:T(8,128)(2,1)} %broadcast_select_fusion), channel_id=1, source_target_pairs={{64,0},{193,1},{128,64},{1,65},{192,128},{65,129},{0,192},{129,193... | collective-permute-start | bytes 4718600 | tf_op jit(solution)/shard_map/ppermute | solution.py:31
  130.3 11.2 %collective-permute-start.14 = (bf16[1,4,64,1024]{3,2,1,0:T(8,128)(2,1)S(1)}, bf16[1,4,64,1024]{3,2,1,0:T(8,128)(2,1)S(1)}, u32[]{:S(2)}, u32[]{:S(2)}) collective-permute-start(bf16[1,4,64,1024]{3,2,1,0:T(8,128)(2,1)S(1)} %collective-permute-done.1.refs_2_), channel_id=1, source_target_pairs={{0,1},{1,0},{2,3},{3,2},{4,5},{5,4},{6,7},{7,6},{8,9},{9,8},{10,11... | collective-permute-start | bytes 1572872 | tf_op jit(solution)/shard_map/ppermute | solution.py:16
  130.3 11.5 %collective-permute-start.16 = (bf16[1,4,64,1024]{3,2,1,0:T(8,128)(2,1)S(1)}, bf16[1,4,64,1024]{3,2,1,0:T(8,128)(2,1)S(1)}, u32[]{:S(2)}, u32[]{:S(2)}) collective-permute-start(bf16[1,4,64,1024]{3,2,1,0:T(8,128)(2,1)S(1)} %collective-permute-done.2.refs_4_), channel_id=1, source_target_pairs={{0,1},{1,0},{2,3},{3,2},{4,5},{5,4},{6,7},{7,6},{8,9},{9,8},{10,11... | collective-permute-start | bytes 1572872 | tf_op jit(solution)/shard_map/ppermute | solution.py:16
  140.1 2.1 collective-permute-start.13
  140.4 2.6 %collective-permute-start.18 = (bf16[1,4,64,1024]{3,2,1,0:T(8,128)(2,1)}, bf16[1,4,64,1024]{3,2,1,0:T(8,128)(2,1)S(1)}, u32[]{:S(2)}, u32[]{:S(2)}) collective-permute-start(bf16[1,4,64,1024]{3,2,1,0:T(8,128)(2,1)} %collective-permute-done.7.refs_6_), channel_id=1, source_target_pairs={{0,1},{1,0},{2,3},{3,2},{4,5},{5,4},{6,7},{7,6},{8,9},{9,8},{10,11... | collective-permute-start | bytes 1572872 | tf_op jit(solution)/shard_map/ppermute | solution.py:16
  141.5 3.6 %collective-permute-start.15 = (bf16[1,4,64,1024]{3,2,1,0:T(8,128)(2,1)S(1)}, bf16[1,4,64,1024]{3,2,1,0:T(8,128)(2,1)S(1)}, u32[]{:S(2)}, u32[]{:S(2)}) collective-permute-start(bf16[1,4,64,1024]{3,2,1,0:T(8,128)(2,1)S(1)} %copy-done.15), channel_id=1, source_target_pairs={{0,1},{1,0},{2,3},{3,2},{4,5},{5,4},{6,7},{7,6},{8,9},{9,8},{10,11... | collective-permute-start | bytes 1572872 | tf_op jit(solution)/shard_map/ppermute | solution.py:16
  141.9 3.2 %collective-permute-start.17 = (bf16[1,4,64,1024]{3,2,1,0:T(8,128)(2,1)S(1)}, bf16[1,4,64,1024]{3,2,1,0:T(8,128)(2,1)S(1)}, u32[]{:S(2)}, u32[]{:S(2)}) collective-permute-start(bf16[1,4,64,1024]{3,2,1,0:T(8,128)(2,1)S(1)} %copy-done.12), channel_id=1, source_target_pairs={{0,1},{1,0},{2,3},{3,2},{4,5},{5,4},{6,7},{7,6},{8,9},{9,8},{10,11... | collective-permute-start | bytes 1572872 | tf_op jit(solution)/shard_map/ppermute | solution.py:16
  142.2 3.1 %collective-permute-start.19 = (bf16[1,4,64,1024]{3,2,1,0:T(8,128)(2,1)}, bf16[1,4,64,1024]{3,2,1,0:T(8,128)(2,1)}, u32[]{:S(2)}, u32[]{:S(2)}) collective-permute-start(bf16[1,4,64,1024]{3,2,1,0:T(8,128)(2,1)} %collective-permute-done.11.refs_7_), channel_id=1, source_target_pairs={{0,1},{1,0},{2,3},{3,2},{4,5},{5,4},{6,7},{7,6},{8,9},{9,8},{10,11... | collective-permute-start | bytes 1572872 | tf_op jit(solution)/shard_map/ppermute | solution.py:16
  143.8 19.2 %collective-permute-start.23 = (bf16[1,1024,256]{2,1,0:T(8,128)(2,1)}, bf16[1,1024,256]{2,1,0:T(8,128)(2,1)}, u32[]{:S(2)}, u32[]{:S(2)}) collective-permute-start(bf16[1,1024,256]{2,1,0:T(8,128)(2,1)} %broadcast_select_fusion.3), channel_id=1, source_target_pairs={{64,0},{193,1},{128,64},{1,65},{192,128},{65,129},{0,192},{129,193... | collective-permute-start | bytes 1572872 | tf_op jit(solution)/shard_map/ppermute | solution.py:31
  145.1 28.6 %copy-start.4 = (f32[1,2048]{1,0:T(1,128)S(1)}, f32[1,2048]{1,0:T(1,128)}, u32[]{:S(2)}) copy-start(f32[1,2048]{1,0:T(1,128)} %p_ref.1) | copy-start | bytes 24580
  187.8 3.1 %collective-permute-start.24 = (f32[8,10,16,256]{3,2,1,0:T(8,128)S(1)}, f32[8,10,16,256]{3,2,1,0:T(8,128)S(1)}, u32[]{:S(2)}, u32[]{:S(2)}) collective-permute-start(f32[8,10,16,256]{3,2,1,0:T(8,128)S(1)} %get-tuple-element.47), channel_id=1, source_target_pairs={{0,1},{1,0},{2,3},{3,2},{4,5},{5,4},{6,7},{7,6},{8,9},{9,8},{10,11... | collective-permute-start | bytes 3932168 | tf_op jit(solution)/shard_map/ppermute | solution.py:16
  228.0 2.1 collective-permute-start.25
  (22 other events, 188.6 us)

commit v4 on v3

--- a/solution.py
+++ b/solution.py
@@ -266,12 +266,12 @@
     barrier = lax.optimization_barrier
     pair = shift(hop_blocks, "zl", 1)
     own_x = [shift(hop_blocks, "x", 1), shift(hop_blocks, "x", 3)]
-    pair, own_x, ring = barrier((pair, own_x, coeffs))
+    values, ring = barrier((split_points(basis_values[0]), coeffs))
     after, before = shift(ring, "zh", 1), shift(ring, "zh", 3)
     pair_x = [shift(pair, "x", 1), shift(pair, "x", 3)]
     own_far = far(*own_x, "x")
     values, after, before, pair_x, own_far = barrier(
-        (split_points(basis_values[0]), after, before, pair_x, own_far)
+        (values, after, before, pair_x, own_far)
     )
 
     values = exchange(values)

time: 236 us -> 231 us (0.979); the launches traced: 232 us -> 230 us
  waiting for transfers between devices: 103 us -> 93.9 us
  starting transfers between devices: 44.9 us -> 52.4 us
    ppermute x11, waiting for transfers between devices: 36.6 us -> 30 us  [shift(): return lax.ppermute(a, axis, [((i + step) % size, i) for i in range(size)])]
    all_to_all x2, starting transfers between devices: 20.3 us -> 24.7 us  [exchange(): return lax.all_to_all(a, GRP, 0, 0, tiled=True)]
    ppermute x5, starting transfers between devices: 5.58 us -> 9.29 us  [far(): return lax.ppermute(held, (axis, 'c'), pairs)]
    unnamed x55 -> x53, local copies, waits for them, and re-layouts: 7.41 us -> 7.82 us
  transfers between devices with their start and end apart: 28 -> 28, of which waited for: 15 -> 14; matrix products, arithmetic and copies ran while one was open for 4% -> 4% of each run, Pallas kernels for 11% -> 11%
where the time goes in v4:
time: 231 us; the launch traced here: 230 us
  waiting for transfers between devices  93.9 us (41%)
  starting transfers between devices  52.4 us (23%)
  blocking collectives  35.8 us (15%)
  Pallas kernels  31.9 us (14%)
  local copies, waits for them, and re-layouts  8.5 us (4%)
  other arithmetic  7.08 us (3%)
    ppermute x5, waiting for transfers between devices, far(): return lax.ppermute(held, (axis, 'c'), pairs)  49.5 us
    ppermute x11, waiting for transfers between devices, shift(): return lax.ppermute(a, axis, [((i + step) % size, i) for i in range(size)])  30 us
    all_to_all x2, starting transfers between devices, exchange(): return lax.all_to_all(a, GRP, 0, 0, tiled=True)  24.7 us
    all_to_all x1, blocking collectives, local(): part = lax.all_to_all(part, CHIPS, 0, 0, tiled=True).astype(jnp.float32)  22 us
    ppermute x11, starting transfers between devices, shift(): return lax.ppermute(a, axis, [((i + step) % size, i) for i in range(size)])  16.1 us
    all_to_all x1, blocking collectives, local(): low = lax.all_to_all(low, CHIPS, 0, 0, tiled=True)  13.9 us
    pallas_call x1, Pallas kernels, hop_apply(): pl.pallas_call(hop_kernel, out_shape=jax.ShapeDtypeStruct((blocks * rows,...  10.7 us
    ppermute x5, starting transfers between devices, far(): return lax.ppermute(held, (axis, 'c'), pairs)  9.29 us
  transfers between devices with their start and end apart: 28, of which 14 were waited for; matrix products, arithmetic and copies ran while one was open for 4% of the time, Pallas kernels for 11%

profile of v4, /device:TPU:80, one launch (start us, length us, event | category | flops | bytes accessed | tf_op | source)
XLA Modules:
  0.0 229.9 jit_solution(4497238955019880654)
XLA Ops:
  0.0 1.5 collective-permute-start.6
  1.5 1.7 collective-permute-start.5
  3.2 1.9 collective-permute-start.2
  5.8 4.4 %split_points.3 = bf16[16,64,2048]{2,1,0:T(8,128)(2,1)} custom-call(bf16[64,32768]{1,0:T(8,128)(2,1)} %bitcast.11), custom_call_target="tpu_custom_call" | custom-call | bytes 8388608 | tf_op jit(solution)/shard_map/split_points/pallas_call | solution.py:49
  10.2 3.7 %collective-permute-start.1 = (bf16[1,1024,256]{2,1,0:T(8,128)(2,1)S(1)}, bf16[1,1024,256]{2,1,0:T(8,128)(2,1)S(1)}, u32[]{:S(2)}, u32[]{:S(2)}) collective-permute-start(bf16[1,1024,256]{2,1,0:T(8,128)(2,1)S(1)} %copy-done.1), channel_id=1, source_target_pairs={{48,0},{0,16},{16,32},{32,48},{49,1},{1,17},{17,33},{33,49},{50,2}... | collective-permute-start | bytes 1572872 | tf_op jit(solution)/shard_map/ppermute | solution.py:21
  15.2 3.0 %collective-permute-start.7 = (bf16[1,4,64,1024]{3,2,1,0:T(8,128)(2,1)S(1)}, bf16[1,4,64,1024]{3,2,1,0:T(8,128)(2,1)S(1)}, u32[]{:S(2)}, u32[]{:S(2)}) collective-permute-start(bf16[1,4,64,1024]{3,2,1,0:T(8,128)(2,1)S(1)} %broadcast_select_fusion.2), channel_id=1, source_target_pairs={{2,0},{7,1},{4,2},{1,3},{6,4},{3,5},{0,6},{5,7},{10,8},{15,9},{12,... | collective-permute-start | bytes 1572872 | tf_op jit(solution)/shard_map/ppermute | solution.py:31
  18.2 11.4 %collective-permute-done.2.refs_1_ = bf16[1,4,64,1024]{3,2,1,0:T(8,128)(2,1)S(1)} collective-permute-done((bf16[1,4,64,1024]{3,2,1,0:T(8,128)(2,1)}, bf16[1,4,64,1024]{3,2,1,0:T(8,128)(2,1)S(1)}, u32[]{:S(2)}, u32[]{:S(2)}) %collective-permute-start.2) | collective-permute-done | bytes 524320 | tf_op jit(solution)/shard_map/ppermute | solution.py:21
  29.8 3.0 %collective-permute-start.3 = (bf16[1,4,64,1024]{3,2,1,0:T(8,128)(2,1)S(1)}, bf16[1,4,64,1024]{3,2,1,0:T(8,128)(2,1)}, u32[]{:S(2)}, u32[]{:S(2)}) collective-permute-start(bf16[1,4,64,1024]{3,2,1,0:T(8,128)(2,1)S(1)} %collective-permute-done.2.refs_1_), channel_id=1, source_target_pairs={{2,0},{4,2},{6,4},{0,6},{3,1},{5,3},{7,5},{1,7},{10,8},{12,10},{14... | collective-permute-start | bytes 1572872 | tf_op jit(solution)/shard_map/ppermute | solution.py:21
  32.8 5.8 %collective-permute-done.1 = bf16[1,1024,256]{2,1,0:T(8,128)(2,1)S(1)} collective-permute-done((bf16[1,1024,256]{2,1,0:T(8,128)(2,1)S(1)}, bf16[1,1024,256]{2,1,0:T(8,128)(2,1)S(1)}, u32[]{:S(2)}, u32[]{:S(2)}) %collective-permute-start.1) | collective-permute-done | bytes 524320 | tf_op jit(solution)/shard_map/ppermute | solution.py:21
  38.6 2.2 collective-permute-done.4.refs_5_
  40.8 6.2 %all-to-all-start.1 = ((bf16[16,64,2048]{2,1,0:T(8,128)(2,1)}), bf16[16,64,2048]{2,1,0:T(8,128)(2,1)}, u32[]{:S(2)}, u32[]{:S(2)}) async-start(bf16[16,64,2048]{2,1,0:T(8,128)(2,1)} %split_points.3), calls=%async_computation.1 | async-start | bytes 8388608 | tf_op jit(solution)/shard_map/all_to_all | solution.py:264
  49.8 1.3 collective-permute-start.10
  51.9 1.9 broadcast_select_fusion.1
  53.8 3.1 %collective-permute-start.11 = (bf16[1,4,64,1024]{3,2,1,0:T(8,128)(2,1)}, bf16[1,4,64,1024]{3,2,1,0:T(8,128)(2,1)}, u32[]{:S(2)}, u32[]{:S(2)}) collective-permute-start(bf16[1,4,64,1024]{3,2,1,0:T(8,128)(2,1)} %broadcast_select_fusion.1), channel_id=1, source_target_pairs={{2,0},{7,1},{4,2},{1,3},{6,4},{3,5},{0,6},{5,7},{10,8},{15,9},{12,... | collective-permute-start | bytes 1572872 | tf_op jit(solution)/shard_map/ppermute | solution.py:31
  56.8 2.2 collective-permute-start.8
  59.0 4.3 %split_points.2 = bf16[16,64,2048]{2,1,0:T(8,128)(2,1)} custom-call(bf16[64,32768]{1,0:T(8,128)(2,1)} %bitcast.12), custom_call_target="tpu_custom_call" | custom-call | bytes 8388608 | tf_op jit(solution)/shard_map/split_points/pallas_call | solution.py:49
  63.3 31.9 %collective-permute-done.11.refs_7_ = bf16[1,4,64,1024]{3,2,1,0:T(8,128)(2,1)} collective-permute-done((bf16[1,4,64,1024]{3,2,1,0:T(8,128)(2,1)}, bf16[1,4,64,1024]{3,2,1,0:T(8,128)(2,1)}, u32[]{:S(2)}, u32[]{:S(2)}) %collective-permute-start.11) | collective-permute-done | bytes 524320 | tf_op jit(solution)/shard_map/ppermute | solution.py:31
  95.3 8.6 %all-to-all-done.1 = bf16[16,64,2048]{2,1,0:T(8,128)(2,1)} async-done(((bf16[16,64,2048]{2,1,0:T(8,128)(2,1)}), bf16[16,64,2048]{2,1,0:T(8,128)(2,1)}, u32[]{:S(2)}, u32[]{:S(2)}) %all-to-all-start.1) | async-done | bytes 4194336 | tf_op jit(solution)/shard_map/all_to_all | solution.py:264
  103.9 18.5 %all-to-all-start = ((bf16[16,64,2048]{2,1,0:T(8,128)(2,1)}), bf16[16,64,2048]{2,1,0:T(8,128)(2,1)}, u32[]{:S(2)}, u32[]{:S(2)}) async-start(bf16[16,64,2048]{2,1,0:T(8,128)(2,1)} %split_points.2), calls=%async_computation | async-start | bytes 8388608 | tf_op jit(solution)/shard_map/all_to_all | solution.py:264
  124.9 2.7 %broadcast_select_fusion = bf16[3,1024,256]{2,1,0:T(8,128)(2,1)} fusion(bf16[3,1024,256]{2,1,0:T(8,128)(2,1)} %collective-permute-done.9.refs_17_, bf16[3,1024,256]{2,1,0:T(8,128)(2,1)S(1)} %collective-permute-done.10.refs_19_, pred[]{:T(512)S(6)} %eq.2), kind=kLoop, calls=%fused_computation | loop fusion | flops 786432 | bytes 4718593 | tf_op jit(solution)/shard_map/jit(_where)/select_n | solution.py:26
  128.7 9.2 %collective-permute-done.22.refs_23_ = bf16[1,1024,256]{2,1,0:T(8,128)(2,1)S(1)} collective-permute-done((bf16[1,1024,256]{2,1,0:T(8,128)(2,1)}, bf16[1,1024,256]{2,1,0:T(8,128)(2,1)S(1)}, u32[]{:S(2)}, u32[]{:S(2)}) %collective-permute-start.22) | collective-permute-done | bytes 524320 | tf_op jit(solution)/shard_map/ppermute | solution.py:21
  143.1 17.5 %collective-permute-done.23.refs_22_ = bf16[1,1024,256]{2,1,0:T(8,128)(2,1)} collective-permute-done((bf16[1,1024,256]{2,1,0:T(8,128)(2,1)}, bf16[1,1024,256]{2,1,0:T(8,128)(2,1)}, u32[]{:S(2)}, u32[]{:S(2)}) %collective-permute-start.23) | collective-permute-done | bytes 524320 | tf_op jit(solution)/shard_map/ppermute | solution.py:31
  161.8 10.7 %hop_apply.1.h_ref = f32[1024,256]{1,0:T(8,128)} custom-call(s32[6]{0:T(128)} %stack.27.pos, s32[16]{0:T(128)} %counts.3, s32[16,4]{1,0:T(8,128)} %copy.8.near, bf16[1,4,64,1024]{3,2,1,0:T(8,128)(2,1)} %refs_0_.1, bf16[1,4,64,1024]{3,2,1,0:T(8,128)(2,1)} %copy-done.13, bf16[1,4,64,1024]{3,2,1,0:T(8,128)(2,1)} %copy-done.9, ...), custom_call_target="tpu_custom_call" | custom-call | flops 2147483648 | bytes 10485760 | tf_op jit(solution)/shard_map/hop_apply/pallas_call | solution.py:193
  172.5 5.1 %value_part.1.g_ref = f32[10,256,256]{2,1,0:T(8,128)S(1)} custom-call(f32[1,2048]{1,0:T(1,128)S(1)} %copy-done.4, bf16[1024,2048]{1,0:T(8,128)(2,1)} %bitcast.8.v_ref), custom_call_target="tpu_custom_call" | custom-call | flops 2684354560 | bytes 6815744 | tf_op jit(solution)/shard_map/value_part/pallas_call | solution.py:82
  177.6 1.5 copy-done.5
  179.1 1.7 copy-done.6
  180.9 5.1 %deriv_part.1 = (f32[8,10,16,256]{3,2,1,0:T(8,128)S(1)}, f32[8,10,16,256]{3,2,1,0:T(8,128)S(1)}) custom-call(s32[6]{0:T(128)S(1)} %copy-done.2, bf16[1024,2048]{1,0:T(8,128)(2,1)} %bitcast.9.d_ref, f32[10,256,256]{2,1,0:T(8,128)S(1)} %copy-done.6), custom_call_target="tpu_custom_call" | custom-call | flops 2684354560 | bytes 9437184 | tf_op jit(solution)/shard_map/deriv_part/pallas_call | solution.py:123
  186.1 3.0 %collective-permute-done.24 = f32[8,10,16,256]{3,2,1,0:T(8,128)S(1)} collective-permute-done((f32[8,10,16,256]{3,2,1,0:T(8,128)S(1)}, f32[8,10,16,256]{3,2,1,0:T(8,128)S(1)}, u32[]{:S(2)}, u32[]{:S(2)}) %collective-permute-start.24) | collective-permute-done | bytes 1310752 | tf_op jit(solution)/shard_map/ppermute | solution.py:16
  189.4 22.0 %all_to_all.20 = bf16[8,10,16,256]{3,2,1,0:T(8,128)(2,1)S(1)} all-to-all(bf16[8,10,16,256]{3,2,1,0:T(8,128)(2,1)S(1)} %add_convert_fusion), channel_id=1, replica_groups=mesh['y'=4,'zh'=4,'zl'=2,'x'=4,'c'=2] {'zl','x'}, dimensions={0} | all-to-all | bytes 1310720 | tf_op jit(solution)/shard_map/all_to_all | solution.py:300
  211.6 13.9 %all_to_all.21.mine_ref = bf16[8,10,16,256]{3,2,1,0:T(8,128)(2,1)S(1)} all-to-all(bf16[8,10,16,256]{3,2,1,0:T(8,128)(2,1)S(1)} %broadcast_in_dim.4), channel_id=1, replica_groups=mesh['y'=4,'zh'=4,'zl'=2,'x'=4,'c'=2] {'zl','x'}, dimensions={0} | all-to-all | bytes 1310720 | tf_op jit(solution)/shard_map/all_to_all | solution.py:304
  225.4 2.1 collective-permute-done.25.other_ref
  227.5 2.3 %own_apply.1 = f32[1024,256]{1,0:T(8,128)} custom-call(s32[6]{0:T(128)S(1)} %copy-done.2, s32[16]{0:T(128)S(1)} %copy-done.3, bf16[8,10,16,256]{3,2,1,0:T(8,128)(2,1)S(1)} %all_to_all.21.mine_ref, bf16[8,10,16,256]{3,2,1,0:T(8,128)(2,1)S(1)} %collective-permute-done.25.other_ref, bf16[1,1024,256]{2,1,0:T(8,128)(2,1)S(1)} %copy-done.1, f32[1024,256]{1,0:T(8,128)S(1)} %copy-done), custom_call_target="tpu_custom_call" | custom-call | flops 536870912 | bytes 3932160 | tf_op jit(solution)/shard_map/own_apply/pallas_call | solution.py:243
  (94 shorter events, 16.3 us)
Async XLA Ops:
  0.0 15.1 %collective-permute-start.6 = (bf16[1,4,64,1024]{3,2,1,0:T(8,128)(2,1)}, bf16[1,4,64,1024]{3,2,1,0:T(8,128)(2,1)S(1)}, u32[]{:S(2)}, u32[]{:S(2)}) collective-permute-start(bf16[1,4,64,1024]{3,2,1,0:T(8,128)(2,1)} %refs_0_.1), channel_id=1, source_target_pairs={{6,0},{0,2},{2,4},{4,6},{7,1},{1,3},{3,5},{5,7},{14,8},{8,10},{10,... | collective-permute-start | bytes 1572872 | tf_op jit(solution)/shard_map/ppermute | solution.py:21
  1.5 13.6 %collective-permute-start.5 = (bf16[1,4,64,1024]{3,2,1,0:T(8,128)(2,1)}, bf16[1,4,64,1024]{3,2,1,0:T(8,128)(2,1)S(1)}, u32[]{:S(2)}, u32[]{:S(2)}) collective-permute-start(bf16[1,4,64,1024]{3,2,1,0:T(8,128)(2,1)} %refs_0_.1), channel_id=1, source_target_pairs={{2,0},{4,2},{6,4},{0,6},{3,1},{5,3},{7,5},{1,7},{10,8},{12,10},{14... | collective-permute-start | bytes 1572872 | tf_op jit(solution)/shard_map/ppermute | solution.py:21
  3.2 26.3 %collective-permute-start.2 = (bf16[1,4,64,1024]{3,2,1,0:T(8,128)(2,1)}, bf16[1,4,64,1024]{3,2,1,0:T(8,128)(2,1)S(1)}, u32[]{:S(2)}, u32[]{:S(2)}) collective-permute-start(bf16[1,4,64,1024]{3,2,1,0:T(8,128)(2,1)} %refs_0_.1), channel_id=1, source_target_pairs={{8,0},{0,8},{9,1},{1,9},{10,2},{2,10},{11,3},{3,11},{12,4},{4,12},... | collective-permute-start | bytes 1572872 | tf_op jit(solution)/shard_map/ppermute | solution.py:21
  10.2 28.4 %collective-permute-start.1 = (bf16[1,1024,256]{2,1,0:T(8,128)(2,1)S(1)}, bf16[1,1024,256]{2,1,0:T(8,128)(2,1)S(1)}, u32[]{:S(2)}, u32[]{:S(2)}) collective-permute-start(bf16[1,1024,256]{2,1,0:T(8,128)(2,1)S(1)} %copy-done.1), channel_id=1, source_target_pairs={{48,0},{0,16},{16,32},{32,48},{49,1},{1,17},{17,33},{33,49},{50,2}... | collective-permute-start | bytes 1572872 | tf_op jit(solution)/shard_map/ppermute | solution.py:21
  13.9 24.7 %collective-permute-start = (bf16[1,1024,256]{2,1,0:T(8,128)(2,1)S(1)}, bf16[1,1024,256]{2,1,0:T(8,128)(2,1)S(1)}, u32[]{:S(2)}, u32[]{:S(2)}) collective-permute-start(bf16[1,1024,256]{2,1,0:T(8,128)(2,1)S(1)} %copy-done.1), channel_id=1, source_target_pairs={{16,0},{32,16},{48,32},{0,48},{17,1},{33,17},{49,33},{1,49},{18,2}... | collective-permute-start | bytes 1572872 | tf_op jit(solution)/shard_map/ppermute | solution.py:21
  15.1 113.0 %copy-start.8 = (bf16[1,4,64,1024]{3,2,1,0:T(8,128)(2,1)}, bf16[1,4,64,1024]{3,2,1,0:T(8,128)(2,1)S(1)}, u32[]{:S(2)}) copy-start(bf16[1,4,64,1024]{3,2,1,0:T(8,128)(2,1)S(1)} %collective-permute-done.6.refs_4_) | copy-start | bytes 1572868
  15.1 113.0 %copy-start.9 = (bf16[1,4,64,1024]{3,2,1,0:T(8,128)(2,1)}, bf16[1,4,64,1024]{3,2,1,0:T(8,128)(2,1)S(1)}, u32[]{:S(2)}) copy-start(bf16[1,4,64,1024]{3,2,1,0:T(8,128)(2,1)S(1)} %collective-permute-done.5.refs_2_) | copy-start | bytes 1572868
  15.2 23.4 %collective-permute-start.7 = (bf16[1,4,64,1024]{3,2,1,0:T(8,128)(2,1)S(1)}, bf16[1,4,64,1024]{3,2,1,0:T(8,128)(2,1)S(1)}, u32[]{:S(2)}, u32[]{:S(2)}) collective-permute-start(bf16[1,4,64,1024]{3,2,1,0:T(8,128)(2,1)S(1)} %broadcast_select_fusion.2), channel_id=1, source_target_pairs={{2,0},{7,1},{4,2},{1,3},{6,4},{3,5},{0,6},{5,7},{10,8},{15,9},{12,... | collective-permute-start | bytes 1572872 | tf_op jit(solution)/shard_map/ppermute | solution.py:31
  29.5 11.3 %collective-permute-start.4 = (bf16[1,4,64,1024]{3,2,1,0:T(8,128)(2,1)S(1)}, bf16[1,4,64,1024]{3,2,1,0:T(8,128)(2,1)}, u32[]{:S(2)}, u32[]{:S(2)}) collective-permute-start(bf16[1,4,64,1024]{3,2,1,0:T(8,128)(2,1)S(1)} %collective-permute-done.2.refs_1_), channel_id=1, source_target_pairs={{6,0},{0,2},{2,4},{4,6},{7,1},{1,3},{3,5},{5,7},{14,8},{8,10},{10,... | collective-permute-start | bytes 1572872 | tf_op jit(solution)/shard_map/ppermute | solution.py:21
  29.8 11.0 %collective-permute-start.3 = (bf16[1,4,64,1024]{3,2,1,0:T(8,128)(2,1)S(1)}, bf16[1,4,64,1024]{3,2,1,0:T(8,128)(2,1)}, u32[]{:S(2)}, u32[]{:S(2)}) collective-permute-start(bf16[1,4,64,1024]{3,2,1,0:T(8,128)(2,1)S(1)} %collective-permute-done.2.refs_1_), channel_id=1, source_target_pairs={{2,0},{4,2},{6,4},{0,6},{3,1},{5,3},{7,5},{1,7},{10,8},{12,10},{14... | collective-permute-start | bytes 1572872 | tf_op jit(solution)/shard_map/ppermute | solution.py:21
  40.8 63.0 %all-to-all-start.1 = ((bf16[16,64,2048]{2,1,0:T(8,128)(2,1)}), bf16[16,64,2048]{2,1,0:T(8,128)(2,1)}, u32[]{:S(2)}, u32[]{:S(2)}) async-start(bf16[16,64,2048]{2,1,0:T(8,128)(2,1)} %split_points.3), calls=%async_computation.1 | async-start | bytes 8388608 | tf_op jit(solution)/shard_map/all_to_all | solution.py:264
  49.8 45.4 %collective-permute-start.10 = (bf16[3,1024,256]{2,1,0:T(8,128)(2,1)}, bf16[3,1024,256]{2,1,0:T(8,128)(2,1)S(1)}, u32[]{:S(2)}, u32[]{:S(2)}) collective-permute-start(bf16[3,1024,256]{2,1,0:T(8,128)(2,1)} %get-tuple-element.45.refs_16_), channel_id=1, source_target_pairs={{192,0},{0,64},{64,128},{128,192},{193,1},{1,65},{65,129},{129,193... | collective-permute-start | bytes 4718600 | tf_op jit(solution)/shard_map/ppermute | solution.py:21
  51.1 44.1 %collective-permute-start.9 = (bf16[3,1024,256]{2,1,0:T(8,128)(2,1)}, bf16[3,1024,256]{2,1,0:T(8,128)(2,1)}, u32[]{:S(2)}, u32[]{:S(2)}) collective-permute-start(bf16[3,1024,256]{2,1,0:T(8,128)(2,1)} %get-tuple-element.45.refs_16_), channel_id=1, source_target_pairs={{64,0},{128,64},{192,128},{0,192},{65,1},{129,65},{193,129},{1,193... | collective-permute-start | bytes 4718600 | tf_op jit(solution)/shard_map/ppermute | solution.py:21
  53.8 41.5 %collective-permute-start.11 = (bf16[1,4,64,1024]{3,2,1,0:T(8,128)(2,1)}, bf16[1,4,64,1024]{3,2,1,0:T(8,128)(2,1)}, u32[]{:S(2)}, u32[]{:S(2)}) collective-permute-start(bf16[1,4,64,1024]{3,2,1,0:T(8,128)(2,1)} %broadcast_select_fusion.1), channel_id=1, source_target_pairs={{2,0},{7,1},{4,2},{1,3},{6,4},{3,5},{0,6},{5,7},{10,8},{15,9},{12,... | collective-permute-start | bytes 1572872 | tf_op jit(solution)/shard_map/ppermute | solution.py:31
  56.8 38.4 %collective-permute-start.8 = (bf16[1,1024,256]{2,1,0:T(8,128)(2,1)}, bf16[1,1024,256]{2,1,0:T(8,128)(2,1)}, u32[]{:S(2)}, u32[]{:S(2)}) collective-permute-start(bf16[1,1024,256]{2,1,0:T(8,128)(2,1)} %get-tuple-element.46), channel_id=1, source_target_pairs={{16,0},{49,1},{32,16},{1,17},{48,32},{17,33},{0,48},{33,49},{18,2}... | collective-permute-start | bytes 1572872 | tf_op jit(solution)/shard_map/ppermute | solution.py:31
  95.3 29.6 %copy-start.7 = (bf16[3,1024,256]{2,1,0:T(8,128)(2,1)}, bf16[3,1024,256]{2,1,0:T(8,128)(2,1)S(1)}, u32[]{:S(2)}) copy-start(bf16[3,1024,256]{2,1,0:T(8,128)(2,1)S(1)} %collective-permute-done.10.refs_19_) | copy-start | bytes 4718596
  103.9 75.2 %all-to-all-start = ((bf16[16,64,2048]{2,1,0:T(8,128)(2,1)}), bf16[16,64,2048]{2,1,0:T(8,128)(2,1)}, u32[]{:S(2)}, u32[]{:S(2)}) async-start(bf16[16,64,2048]{2,1,0:T(8,128)(2,1)} %split_points.2), calls=%async_computation | async-start | bytes 8388608 | tf_op jit(solution)/shard_map/all_to_all | solution.py:264
  122.4 5.7 %collective-permute-start.12 = (bf16[1,4,64,1024]{3,2,1,0:T(8,128)(2,1)}, bf16[1,4,64,1024]{3,2,1,0:T(8,128)(2,1)S(1)}, u32[]{:S(2)}, u32[]{:S(2)}) collective-permute-start(bf16[1,4,64,1024]{3,2,1,0:T(8,128)(2,1)} %refs_0_.1), channel_id=1, source_target_pairs={{0,1},{1,0},{2,3},{3,2},{4,5},{5,4},{6,7},{7,6},{8,9},{9,8},{10,11... | collective-permute-start | bytes 1572872 | tf_op jit(solution)/shard_map/ppermute | solution.py:16
  122.9 15.0 %collective-permute-start.22 = (bf16[1,1024,256]{2,1,0:T(8,128)(2,1)}, bf16[1,1024,256]{2,1,0:T(8,128)(2,1)S(1)}, u32[]{:S(2)}, u32[]{:S(2)}) collective-permute-start(bf16[1,1024,256]{2,1,0:T(8,128)(2,1)} %collective-permute-done.8.refs_20_), channel_id=1, source_target_pairs={{192,0},{0,64},{64,128},{128,192},{193,1},{1,65},{65,129},{129,193... | collective-permute-start | bytes 1572872 | tf_op jit(solution)/shard_map/ppermute | solution.py:21
  124.1 13.9 %collective-permute-start.21 = (bf16[1,1024,256]{2,1,0:T(8,128)(2,1)}, bf16[1,1024,256]{2,1,0:T(8,128)(2,1)S(1)}, u32[]{:S(2)}, u32[]{:S(2)}) collective-permute-start(bf16[1,1024,256]{2,1,0:T(8,128)(2,1)} %collective-permute-done.8.refs_20_), channel_id=1, source_target_pairs={{64,0},{128,64},{192,128},{0,192},{65,1},{129,65},{193,129},{1,193... | collective-permute-start | bytes 1572872 | tf_op jit(solution)/shard_map/ppermute | solution.py:21
  127.6 33.0 %collective-permute-start.20 = (bf16[3,1024,256]{2,1,0:T(8,128)(2,1)}, bf16[3,1024,256]{2,1,0:T(8,128)(2,1)S(1)}, u32[]{:S(2)}, u32[]{:S(2)}) collective-permute-start(bf16[3,1024,256]{2,1,0:T(8,128)(2,1)} %broadcast_select_fusion), channel_id=1, source_target_pairs={{64,0},{193,1},{128,64},{1,65},{192,128},{65,129},{0,192},{129,193... | collective-permute-start | bytes 4718600 | tf_op jit(solution)/shard_map/ppermute | solution.py:31
  128.1 11.2 %collective-permute-start.16 = (bf16[1,4,64,1024]{3,2,1,0:T(8,128)(2,1)S(1)}, bf16[1,4,64,1024]{3,2,1,0:T(8,128)(2,1)S(1)}, u32[]{:S(2)}, u32[]{:S(2)}) collective-permute-start(bf16[1,4,64,1024]{3,2,1,0:T(8,128)(2,1)S(1)} %collective-permute-done.6.refs_4_), channel_id=1, source_target_pairs={{0,1},{1,0},{2,3},{3,2},{4,5},{5,4},{6,7},{7,6},{8,9},{9,8},{10,11... | collective-permute-start | bytes 1572872 | tf_op jit(solution)/shard_map/ppermute | solution.py:16
  128.1 11.3 %collective-permute-start.14 = (bf16[1,4,64,1024]{3,2,1,0:T(8,128)(2,1)S(1)}, bf16[1,4,64,1024]{3,2,1,0:T(8,128)(2,1)S(1)}, u32[]{:S(2)}, u32[]{:S(2)}) collective-permute-start(bf16[1,4,64,1024]{3,2,1,0:T(8,128)(2,1)S(1)} %collective-permute-done.5.refs_2_), channel_id=1, source_target_pairs={{0,1},{1,0},{2,3},{3,2},{4,5},{5,4},{6,7},{7,6},{8,9},{9,8},{10,11... | collective-permute-start | bytes 1572872 | tf_op jit(solution)/shard_map/ppermute | solution.py:16
  137.8 2.1 collective-permute-start.13
  138.1 2.4 %collective-permute-start.18 = (bf16[1,4,64,1024]{3,2,1,0:T(8,128)(2,1)S(1)}, bf16[1,4,64,1024]{3,2,1,0:T(8,128)(2,1)S(1)}, u32[]{:S(2)}, u32[]{:S(2)}) collective-permute-start(bf16[1,4,64,1024]{3,2,1,0:T(8,128)(2,1)S(1)} %copy-done.16), channel_id=1, source_target_pairs={{0,1},{1,0},{2,3},{3,2},{4,5},{5,4},{6,7},{7,6},{8,9},{9,8},{10,11... | collective-permute-start | bytes 1572872 | tf_op jit(solution)/shard_map/ppermute | solution.py:16
  139.3 3.5 %collective-permute-start.15 = (bf16[1,4,64,1024]{3,2,1,0:T(8,128)(2,1)}, bf16[1,4,64,1024]{3,2,1,0:T(8,128)(2,1)S(1)}, u32[]{:S(2)}, u32[]{:S(2)}) collective-permute-start(bf16[1,4,64,1024]{3,2,1,0:T(8,128)(2,1)} %collective-permute-done.3.refs_3_), channel_id=1, source_target_pairs={{0,1},{1,0},{2,3},{3,2},{4,5},{5,4},{6,7},{7,6},{8,9},{9,8},{10,11... | collective-permute-start | bytes 1572872 | tf_op jit(solution)/shard_map/ppermute | solution.py:16
  139.4 3.5 %collective-permute-start.17 = (bf16[1,4,64,1024]{3,2,1,0:T(8,128)(2,1)}, bf16[1,4,64,1024]{3,2,1,0:T(8,128)(2,1)S(1)}, u32[]{:S(2)}, u32[]{:S(2)}) collective-permute-start(bf16[1,4,64,1024]{3,2,1,0:T(8,128)(2,1)} %collective-permute-done.4.refs_5_), channel_id=1, source_target_pairs={{0,1},{1,0},{2,3},{3,2},{4,5},{5,4},{6,7},{7,6},{8,9},{9,8},{10,11... | collective-permute-start | bytes 1572872 | tf_op jit(solution)/shard_map/ppermute | solution.py:16
  139.9 3.2 %collective-permute-start.19 = (bf16[1,4,64,1024]{3,2,1,0:T(8,128)(2,1)}, bf16[1,4,64,1024]{3,2,1,0:T(8,128)(2,1)}, u32[]{:S(2)}, u32[]{:S(2)}) collective-permute-start(bf16[1,4,64,1024]{3,2,1,0:T(8,128)(2,1)} %collective-permute-done.11.refs_7_), channel_id=1, source_target_pairs={{0,1},{1,0},{2,3},{3,2},{4,5},{5,4},{6,7},{7,6},{8,9},{9,8},{10,11... | collective-permute-start | bytes 1572872 | tf_op jit(solution)/shard_map/ppermute | solution.py:16
  141.5 19.1 %collective-permute-start.23 = (bf16[1,1024,256]{2,1,0:T(8,128)(2,1)}, bf16[1,1024,256]{2,1,0:T(8,128)(2,1)}, u32[]{:S(2)}, u32[]{:S(2)}) collective-permute-start(bf16[1,1024,256]{2,1,0:T(8,128)(2,1)} %broadcast_select_fusion.3), channel_id=1, source_target_pairs={{64,0},{193,1},{128,64},{1,65},{192,128},{65,129},{0,192},{129,193... | collective-permute-start | bytes 1572872 | tf_op jit(solution)/shard_map/ppermute | solution.py:31
  142.8 29.7 %copy-start.4 = (f32[1,2048]{1,0:T(1,128)S(1)}, f32[1,2048]{1,0:T(1,128)}, u32[]{:S(2)}) copy-start(f32[1,2048]{1,0:T(1,128)} %p_ref.1) | copy-start | bytes 24580
  186.0 3.1 %collective-permute-start.24 = (f32[8,10,16,256]{3,2,1,0:T(8,128)S(1)}, f32[8,10,16,256]{3,2,1,0:T(8,128)S(1)}, u32[]{:S(2)}, u32[]{:S(2)}) collective-permute-start(f32[8,10,16,256]{3,2,1,0:T(8,128)S(1)} %get-tuple-element.43), channel_id=1, source_target_pairs={{0,1},{1,0},{2,3},{3,2},{4,5},{5,4},{6,7},{7,6},{8,9},{9,8},{10,11... | collective-permute-start | bytes 3932168 | tf_op jit(solution)/shard_map/ppermute | solution.py:16
  225.4 2.1 collective-permute-start.25
  (21 other events, 162.1 us)

commit v5 on v4

--- a/solution.py
+++ b/solution.py
@@ -284,6 +284,9 @@
     )
 
     derivs = exchange(derivs)
+    width = coeffs.shape[1]
+    part = value_part(potential, values.reshape(width, -1))
+    part, opposite, near_y = barrier((part, opposite, near_y))
     far_y = far(*near_y, "y")
     near_o = [shift(opposite, "y", 1), shift(opposite, "y", 3)]
     pieces = [stacked, near_y[0], far_y, near_y[1]]
@@ -291,8 +294,6 @@
     hops = [hop_blocks, pair, own_x[0], pair_x[0], own_x[1], pair_x[1], own_far, pair_far]
     others = [swap_cores(h) for h in hops]
     hopped = hop_apply(pos, counts, neighbours, hops + others, pieces)
-    width = coeffs.shape[1]
-    part = value_part(potential, values.reshape(width, -1))
     derivs, hopped, part = barrier((derivs, hopped, part))
 
     keep, send = deriv_part(pos, derivs.reshape(width, -1), part)

time: 231 us -> 233 us (level)
  waiting for transfers between devices: 93.9 us -> 101 us
  starting transfers between devices: 52.4 us -> 47.8 us
    ppermute x11, waiting for transfers between devices: 30 us -> 36.1 us  [shift(): return lax.ppermute(a, axis, [((i + step) % size, i) for i in range(size)])]
    ppermute x5, starting transfers between devices: 9.29 us -> 5.24 us  [far(): return lax.ppermute(held, (axis, 'c'), pairs)]
    unnamed x53 -> x47, local copies, waits for them, and re-layouts: 7.82 us -> 6.42 us
  transfers between devices with their start and end apart: 28 -> 28, of which waited for: 14 -> 15; matrix products, arithmetic and copies ran while one was open for 4% -> 4% of each run, Pallas kernels for 11% -> 10%
where the time goes in v5:
time: 233 us; the launch traced here: 232 us
  waiting for transfers between devices  101 us (43%)
  starting transfers between devices  47.8 us (21%)
  blocking collectives  36.3 us (16%)
  Pallas kernels  31.8 us (14%)
  other arithmetic  7.24 us (3%)
  local copies, waits for them, and re-layouts  7.12 us (3%)
    ppermute x5, waiting for transfers between devices, far(): return lax.ppermute(held, (axis, 'c'), pairs)  50.4 us
    ppermute x11, waiting for transfers between devices, shift(): return lax.ppermute(a, axis, [((i + step) % size, i) for i in range(size)])  36.1 us
    all_to_all x2, starting transfers between devices, exchange(): return lax.all_to_all(a, GRP, 0, 0, tiled=True)  24.2 us
    all_to_all x1, blocking collectives, local(): part = lax.all_to_all(part, CHIPS, 0, 0, tiled=True).astype(jnp.float32)  22.5 us
    ppermute x11, starting transfers between devices, shift(): return lax.ppermute(a, axis, [((i + step) % size, i) for i in range(size)])  16.3 us
    all_to_all x1, blocking collectives, local(): low = lax.all_to_all(low, CHIPS, 0, 0, tiled=True)  13.9 us
    pallas_call x1, Pallas kernels, hop_apply(): pl.pallas_call(hop_kernel, out_shape=jax.ShapeDtypeStruct((blocks * rows,...  10.7 us
    all_to_all x2, waiting for transfers between devices, exchange(): return lax.all_to_all(a, GRP, 0, 0, tiled=True)  9.67 us
  transfers between devices with their start and end apart: 28, of which 15 were waited for; matrix products, arithmetic and copies ran while one was open for 4% of the time, Pallas kernels for 10%

profile of v5, /device:TPU:80, one launch (start us, length us, event | category | flops | bytes accessed | tf_op | source)
XLA Modules:
  0.0 232.0 jit_solution(14747133179373802197)
XLA Ops:
  0.0 2.8 %collective-permute-start.5 = (bf16[1,4,64,1024]{3,2,1,0:T(8,128)(2,1)}, bf16[1,4,64,1024]{3,2,1,0:T(8,128)(2,1)S(1)}, u32[]{:S(2)}, u32[]{:S(2)}) collective-permute-start(bf16[1,4,64,1024]{3,2,1,0:T(8,128)(2,1)} %refs_0_.1), channel_id=1, source_target_pairs={{2,0},{4,2},{6,4},{0,6},{3,1},{5,3},{7,5},{1,7},{10,8},{12,10},{14... | collective-permute-start | bytes 1572872 | tf_op jit(solution)/shard_map/ppermute | solution.py:21
  2.8 1.9 collective-permute-start.2
  5.3 4.3 %split_points.3 = bf16[16,64,2048]{2,1,0:T(8,128)(2,1)} custom-call(bf16[64,32768]{1,0:T(8,128)(2,1)} %bitcast.11), custom_call_target="tpu_custom_call" | custom-call | bytes 8388608 | tf_op jit(solution)/shard_map/split_points/pallas_call | solution.py:49
  9.8 4.1 %collective-permute-start.1 = (bf16[1,1024,256]{2,1,0:T(8,128)(2,1)S(1)}, bf16[1,1024,256]{2,1,0:T(8,128)(2,1)S(1)}, u32[]{:S(2)}, u32[]{:S(2)}) collective-permute-start(bf16[1,1024,256]{2,1,0:T(8,128)(2,1)S(1)} %copy-done.1), channel_id=1, source_target_pairs={{48,0},{0,16},{16,32},{32,48},{49,1},{1,17},{17,33},{33,49},{50,2}... | collective-permute-start | bytes 1572872 | tf_op jit(solution)/shard_map/ppermute | solution.py:21
  14.3 3.3 %collective-permute-done.6.refs_4_ = bf16[1,4,64,1024]{3,2,1,0:T(8,128)(2,1)S(1)} collective-permute-done((bf16[1,4,64,1024]{3,2,1,0:T(8,128)(2,1)}, bf16[1,4,64,1024]{3,2,1,0:T(8,128)(2,1)S(1)}, u32[]{:S(2)}, u32[]{:S(2)}) %collective-permute-start.6) | collective-permute-done | bytes 524320 | tf_op jit(solution)/shard_map/ppermute | solution.py:21
  18.0 11.0 %collective-permute-done.2.refs_1_ = bf16[1,4,64,1024]{3,2,1,0:T(8,128)(2,1)S(1)} collective-permute-done((bf16[1,4,64,1024]{3,2,1,0:T(8,128)(2,1)}, bf16[1,4,64,1024]{3,2,1,0:T(8,128)(2,1)S(1)}, u32[]{:S(2)}, u32[]{:S(2)}) %collective-permute-start.2) | collective-permute-done | bytes 524320 | tf_op jit(solution)/shard_map/ppermute | solution.py:21
  29.0 3.3 %collective-permute-start.3 = (bf16[1,4,64,1024]{3,2,1,0:T(8,128)(2,1)S(1)}, bf16[1,4,64,1024]{3,2,1,0:T(8,128)(2,1)}, u32[]{:S(2)}, u32[]{:S(2)}) collective-permute-start(bf16[1,4,64,1024]{3,2,1,0:T(8,128)(2,1)S(1)} %collective-permute-done.2.refs_1_), channel_id=1, source_target_pairs={{2,0},{4,2},{6,4},{0,6},{3,1},{5,3},{7,5},{1,7},{10,8},{12,10},{14... | collective-permute-start | bytes 1572872 | tf_op jit(solution)/shard_map/ppermute | solution.py:21
  32.3 6.1 %collective-permute-done.1 = bf16[1,1024,256]{2,1,0:T(8,128)(2,1)S(1)} collective-permute-done((bf16[1,1024,256]{2,1,0:T(8,128)(2,1)S(1)}, bf16[1,1024,256]{2,1,0:T(8,128)(2,1)S(1)}, u32[]{:S(2)}, u32[]{:S(2)}) %collective-permute-start.1) | collective-permute-done | bytes 524320 | tf_op jit(solution)/shard_map/ppermute | solution.py:21
  38.4 2.4 %collective-permute-done.3.refs_3_ = bf16[1,4,64,1024]{3,2,1,0:T(8,128)(2,1)} collective-permute-done((bf16[1,4,64,1024]{3,2,1,0:T(8,128)(2,1)S(1)}, bf16[1,4,64,1024]{3,2,1,0:T(8,128)(2,1)}, u32[]{:S(2)}, u32[]{:S(2)}) %collective-permute-start.3) | collective-permute-done | bytes 524320 | tf_op jit(solution)/shard_map/ppermute | solution.py:21
  40.8 3.4 %collective-permute-done.4.refs_5_ = bf16[1,4,64,1024]{3,2,1,0:T(8,128)(2,1)} collective-permute-done((bf16[1,4,64,1024]{3,2,1,0:T(8,128)(2,1)S(1)}, bf16[1,4,64,1024]{3,2,1,0:T(8,128)(2,1)}, u32[]{:S(2)}, u32[]{:S(2)}) %collective-permute-start.4) | collective-permute-done | bytes 524320 | tf_op jit(solution)/shard_map/ppermute | solution.py:21
  44.2 4.6 %all-to-all-start.1 = ((bf16[16,64,2048]{2,1,0:T(8,128)(2,1)}), bf16[16,64,2048]{2,1,0:T(8,128)(2,1)}, u32[]{:S(2)}, u32[]{:S(2)}) async-start(bf16[16,64,2048]{2,1,0:T(8,128)(2,1)} %split_points.3), calls=%async_computation.1 | async-start | bytes 8388608 | tf_op jit(solution)/shard_map/all_to_all | solution.py:264
  53.6 1.9 broadcast_select_fusion.1
  55.5 3.0 %collective-permute-start.11 = (bf16[1,4,64,1024]{3,2,1,0:T(8,128)(2,1)}, bf16[1,4,64,1024]{3,2,1,0:T(8,128)(2,1)}, u32[]{:S(2)}, u32[]{:S(2)}) collective-permute-start(bf16[1,4,64,1024]{3,2,1,0:T(8,128)(2,1)} %broadcast_select_fusion.1), channel_id=1, source_target_pairs={{2,0},{7,1},{4,2},{1,3},{6,4},{3,5},{0,6},{5,7},{10,8},{15,9},{12,... | collective-permute-start | bytes 1572872 | tf_op jit(solution)/shard_map/ppermute | solution.py:31
  58.5 4.2 %split_points.2 = bf16[16,64,2048]{2,1,0:T(8,128)(2,1)} custom-call(bf16[64,32768]{1,0:T(8,128)(2,1)} %bitcast.12), custom_call_target="tpu_custom_call" | custom-call | bytes 8388608 | tf_op jit(solution)/shard_map/split_points/pallas_call | solution.py:49
  62.7 34.1 %collective-permute-done.11.refs_7_ = bf16[1,4,64,1024]{3,2,1,0:T(8,128)(2,1)} collective-permute-done((bf16[1,4,64,1024]{3,2,1,0:T(8,128)(2,1)}, bf16[1,4,64,1024]{3,2,1,0:T(8,128)(2,1)}, u32[]{:S(2)}, u32[]{:S(2)}) %collective-permute-start.11) | collective-permute-done | bytes 524320 | tf_op jit(solution)/shard_map/ppermute | solution.py:31
  96.9 8.0 %all-to-all-done.1 = bf16[16,64,2048]{2,1,0:T(8,128)(2,1)} async-done(((bf16[16,64,2048]{2,1,0:T(8,128)(2,1)}), bf16[16,64,2048]{2,1,0:T(8,128)(2,1)}, u32[]{:S(2)}, u32[]{:S(2)}) %all-to-all-start.1) | async-done | bytes 4194336 | tf_op jit(solution)/shard_map/all_to_all | solution.py:264
  104.9 19.6 %all-to-all-start = ((bf16[16,64,2048]{2,1,0:T(8,128)(2,1)}), bf16[16,64,2048]{2,1,0:T(8,128)(2,1)}, u32[]{:S(2)}, u32[]{:S(2)}) async-start(bf16[16,64,2048]{2,1,0:T(8,128)(2,1)} %split_points.2), calls=%async_computation | async-start | bytes 8388608 | tf_op jit(solution)/shard_map/all_to_all | solution.py:264
  124.8 5.1 %value_part.1.g_ref = f32[10,256,256]{2,1,0:T(8,128)S(1)} custom-call(f32[1,2048]{1,0:T(1,128)S(1)} %copy-done.4, bf16[1024,2048]{1,0:T(8,128)(2,1)} %bitcast.8.v_ref), custom_call_target="tpu_custom_call" | custom-call | flops 2684354560 | bytes 6815744 | tf_op jit(solution)/shard_map/value_part/pallas_call | solution.py:82
  130.5 1.6 collective-permute-start.22
  132.1 2.8 %broadcast_select_fusion = bf16[3,1024,256]{2,1,0:T(8,128)(2,1)} fusion(bf16[3,1024,256]{2,1,0:T(8,128)(2,1)} %collective-permute-done.9.refs_17_, bf16[3,1024,256]{2,1,0:T(8,128)(2,1)S(1)} %collective-permute-done.10.refs_19_, pred[]{:T(512)S(6)} %eq.2), kind=kLoop, calls=%fused_computation | loop fusion | flops 786432 | bytes 4718593 | tf_op jit(solution)/shard_map/jit(_where)/select_n | solution.py:26
  136.0 8.6 %collective-permute-done.21.refs_21_ = bf16[1,1024,256]{2,1,0:T(8,128)(2,1)S(1)} collective-permute-done((bf16[1,1024,256]{2,1,0:T(8,128)(2,1)}, bf16[1,1024,256]{2,1,0:T(8,128)(2,1)S(1)}, u32[]{:S(2)}, u32[]{:S(2)}) %collective-permute-start.21) | collective-permute-done | bytes 524320 | tf_op jit(solution)/shard_map/ppermute | solution.py:21
  148.6 1.4 collective-permute-start.23
  150.8 16.3 %collective-permute-done.23.refs_22_ = bf16[1,1024,256]{2,1,0:T(8,128)(2,1)} collective-permute-done((bf16[1,1024,256]{2,1,0:T(8,128)(2,1)}, bf16[1,1024,256]{2,1,0:T(8,128)(2,1)}, u32[]{:S(2)}, u32[]{:S(2)}) %collective-permute-start.23) | collective-permute-done | bytes 524320 | tf_op jit(solution)/shard_map/ppermute | solution.py:31
  168.4 10.7 %hop_apply.1.h_ref = f32[1024,256]{1,0:T(8,128)} custom-call(s32[6]{0:T(128)} %stack.27.pos, s32[16]{0:T(128)} %counts.3, s32[16,4]{1,0:T(8,128)} %copy.8.near, bf16[1,4,64,1024]{3,2,1,0:T(8,128)(2,1)} %refs_0_.1, bf16[1,4,64,1024]{3,2,1,0:T(8,128)(2,1)} %copy-done.13, bf16[1,4,64,1024]{3,2,1,0:T(8,128)(2,1)} %copy-done.8, ...), custom_call_target="tpu_custom_call" | custom-call | flops 2147483648 | bytes 10485760 | tf_op jit(solution)/shard_map/hop_apply/pallas_call | solution.py:193
  179.0 1.7 all-to-all-done
  180.7 1.7 copy-done.6
  182.4 5.1 %deriv_part.1 = (f32[8,10,16,256]{3,2,1,0:T(8,128)S(1)}, f32[8,10,16,256]{3,2,1,0:T(8,128)S(1)}) custom-call(s32[6]{0:T(128)S(1)} %copy-done.2, bf16[1024,2048]{1,0:T(8,128)(2,1)} %bitcast.9.d_ref, f32[10,256,256]{2,1,0:T(8,128)S(1)} %copy-done.6), custom_call_target="tpu_custom_call" | custom-call | flops 2684354560 | bytes 9437184 | tf_op jit(solution)/shard_map/deriv_part/pallas_call | solution.py:123
  187.7 3.0 %collective-permute-done.24 = f32[8,10,16,256]{3,2,1,0:T(8,128)S(1)} collective-permute-done((f32[8,10,16,256]{3,2,1,0:T(8,128)S(1)}, f32[8,10,16,256]{3,2,1,0:T(8,128)S(1)}, u32[]{:S(2)}, u32[]{:S(2)}) %collective-permute-start.24) | collective-permute-done | bytes 1310752 | tf_op jit(solution)/shard_map/ppermute | solution.py:16
  191.0 22.5 %all_to_all.20 = bf16[8,10,16,256]{3,2,1,0:T(8,128)(2,1)S(1)} all-to-all(bf16[8,10,16,256]{3,2,1,0:T(8,128)(2,1)S(1)} %add_convert_fusion), channel_id=1, replica_groups=mesh['y'=4,'zh'=4,'zl'=2,'x'=4,'c'=2] {'zl','x'}, dimensions={0} | all-to-all | bytes 1310720 | tf_op jit(solution)/shard_map/all_to_all | solution.py:301
  213.6 13.9 %all_to_all.21.mine_ref = bf16[8,10,16,256]{3,2,1,0:T(8,128)(2,1)S(1)} all-to-all(bf16[8,10,16,256]{3,2,1,0:T(8,128)(2,1)S(1)} %broadcast_in_dim.4), channel_id=1, replica_groups=mesh['y'=4,'zh'=4,'zl'=2,'x'=4,'c'=2] {'zl','x'}, dimensions={0} | all-to-all | bytes 1310720 | tf_op jit(solution)/shard_map/all_to_all | solution.py:305
  227.5 2.1 collective-permute-done.25.other_ref
  229.6 2.3 %own_apply.1 = f32[1024,256]{1,0:T(8,128)} custom-call(s32[6]{0:T(128)S(1)} %copy-done.2, s32[16]{0:T(128)S(1)} %copy-done.3, bf16[8,10,16,256]{3,2,1,0:T(8,128)(2,1)S(1)} %all_to_all.21.mine_ref, bf16[8,10,16,256]{3,2,1,0:T(8,128)(2,1)S(1)} %collective-permute-done.25.other_ref, bf16[1,1024,256]{2,1,0:T(8,128)(2,1)S(1)} %copy-done.1, f32[1024,256]{1,0:T(8,128)S(1)} %copy-done), custom_call_target="tpu_custom_call" | custom-call | flops 536870912 | bytes 3932160 | tf_op jit(solution)/shard_map/own_apply/pallas_call | solution.py:243
  (88 shorter events, 14.9 us)
Async XLA Ops:
  0.0 14.3 %collective-permute-start.5 = (bf16[1,4,64,1024]{3,2,1,0:T(8,128)(2,1)}, bf16[1,4,64,1024]{3,2,1,0:T(8,128)(2,1)S(1)}, u32[]{:S(2)}, u32[]{:S(2)}) collective-permute-start(bf16[1,4,64,1024]{3,2,1,0:T(8,128)(2,1)} %refs_0_.1), channel_id=1, source_target_pairs={{2,0},{4,2},{6,4},{0,6},{3,1},{5,3},{7,5},{1,7},{10,8},{12,10},{14... | collective-permute-start | bytes 1572872 | tf_op jit(solution)/shard_map/ppermute | solution.py:21
  2.8 14.8 %collective-permute-start.6 = (bf16[1,4,64,1024]{3,2,1,0:T(8,128)(2,1)}, bf16[1,4,64,1024]{3,2,1,0:T(8,128)(2,1)S(1)}, u32[]{:S(2)}, u32[]{:S(2)}) collective-permute-start(bf16[1,4,64,1024]{3,2,1,0:T(8,128)(2,1)} %refs_0_.1), channel_id=1, source_target_pairs={{6,0},{0,2},{2,4},{4,6},{7,1},{1,3},{3,5},{5,7},{14,8},{8,10},{10,... | collective-permute-start | bytes 1572872 | tf_op jit(solution)/shard_map/ppermute | solution.py:21
  2.8 26.3 %collective-permute-start.2 = (bf16[1,4,64,1024]{3,2,1,0:T(8,128)(2,1)}, bf16[1,4,64,1024]{3,2,1,0:T(8,128)(2,1)S(1)}, u32[]{:S(2)}, u32[]{:S(2)}) collective-permute-start(bf16[1,4,64,1024]{3,2,1,0:T(8,128)(2,1)} %refs_0_.1), channel_id=1, source_target_pairs={{8,0},{0,8},{9,1},{1,9},{10,2},{2,10},{11,3},{3,11},{12,4},{4,12},... | collective-permute-start | bytes 1572872 | tf_op jit(solution)/shard_map/ppermute | solution.py:21
  9.7 22.6 %collective-permute-start = (bf16[1,1024,256]{2,1,0:T(8,128)(2,1)S(1)}, bf16[1,1024,256]{2,1,0:T(8,128)(2,1)S(1)}, u32[]{:S(2)}, u32[]{:S(2)}) collective-permute-start(bf16[1,1024,256]{2,1,0:T(8,128)(2,1)S(1)} %copy-done.1), channel_id=1, source_target_pairs={{16,0},{32,16},{48,32},{0,48},{17,1},{33,17},{49,33},{1,49},{18,2}... | collective-permute-start | bytes 1572872 | tf_op jit(solution)/shard_map/ppermute | solution.py:21
  9.8 28.6 %collective-permute-start.1 = (bf16[1,1024,256]{2,1,0:T(8,128)(2,1)S(1)}, bf16[1,1024,256]{2,1,0:T(8,128)(2,1)S(1)}, u32[]{:S(2)}, u32[]{:S(2)}) collective-permute-start(bf16[1,1024,256]{2,1,0:T(8,128)(2,1)S(1)} %copy-done.1), channel_id=1, source_target_pairs={{48,0},{0,16},{16,32},{32,48},{49,1},{1,17},{17,33},{33,49},{50,2}... | collective-permute-start | bytes 1572872 | tf_op jit(solution)/shard_map/ppermute | solution.py:21
  14.3 121.3 %copy-start.8 = (bf16[1,4,64,1024]{3,2,1,0:T(8,128)(2,1)}, bf16[1,4,64,1024]{3,2,1,0:T(8,128)(2,1)S(1)}, u32[]{:S(2)}) copy-start(bf16[1,4,64,1024]{3,2,1,0:T(8,128)(2,1)S(1)} %collective-permute-done.5.refs_2_) | copy-start | bytes 1572868
  17.6 127.0 %copy-start.9 = (bf16[1,4,64,1024]{3,2,1,0:T(8,128)(2,1)}, bf16[1,4,64,1024]{3,2,1,0:T(8,128)(2,1)S(1)}, u32[]{:S(2)}) copy-start(bf16[1,4,64,1024]{3,2,1,0:T(8,128)(2,1)S(1)} %collective-permute-done.6.refs_4_) | copy-start | bytes 1572868
  17.6 20.7 %collective-permute-start.7 = (bf16[1,4,64,1024]{3,2,1,0:T(8,128)(2,1)S(1)}, bf16[1,4,64,1024]{3,2,1,0:T(8,128)(2,1)}, u32[]{:S(2)}, u32[]{:S(2)}) collective-permute-start(bf16[1,4,64,1024]{3,2,1,0:T(8,128)(2,1)S(1)} %broadcast_select_fusion.2), channel_id=1, source_target_pairs={{2,0},{7,1},{4,2},{1,3},{6,4},{3,5},{0,6},{5,7},{10,8},{15,9},{12,... | collective-permute-start | bytes 1572872 | tf_op jit(solution)/shard_map/ppermute | solution.py:31
  29.0 11.8 %collective-permute-start.3 = (bf16[1,4,64,1024]{3,2,1,0:T(8,128)(2,1)S(1)}, bf16[1,4,64,1024]{3,2,1,0:T(8,128)(2,1)}, u32[]{:S(2)}, u32[]{:S(2)}) collective-permute-start(bf16[1,4,64,1024]{3,2,1,0:T(8,128)(2,1)S(1)} %collective-permute-done.2.refs_1_), channel_id=1, source_target_pairs={{2,0},{4,2},{6,4},{0,6},{3,1},{5,3},{7,5},{1,7},{10,8},{12,10},{14... | collective-permute-start | bytes 1572872 | tf_op jit(solution)/shard_map/ppermute | solution.py:21
  32.3 11.9 %collective-permute-start.4 = (bf16[1,4,64,1024]{3,2,1,0:T(8,128)(2,1)S(1)}, bf16[1,4,64,1024]{3,2,1,0:T(8,128)(2,1)}, u32[]{:S(2)}, u32[]{:S(2)}) collective-permute-start(bf16[1,4,64,1024]{3,2,1,0:T(8,128)(2,1)S(1)} %collective-permute-done.2.refs_1_), channel_id=1, source_target_pairs={{6,0},{0,2},{2,4},{4,6},{7,1},{1,3},{3,5},{5,7},{14,8},{8,10},{10,... | collective-permute-start | bytes 1572872 | tf_op jit(solution)/shard_map/ppermute | solution.py:21
  44.2 60.7 %all-to-all-start.1 = ((bf16[16,64,2048]{2,1,0:T(8,128)(2,1)}), bf16[16,64,2048]{2,1,0:T(8,128)(2,1)}, u32[]{:S(2)}, u32[]{:S(2)}) async-start(bf16[16,64,2048]{2,1,0:T(8,128)(2,1)} %split_points.3), calls=%async_computation.1 | async-start | bytes 8388608 | tf_op jit(solution)/shard_map/all_to_all | solution.py:264
  51.6 45.3 %collective-permute-start.10 = (bf16[3,1024,256]{2,1,0:T(8,128)(2,1)}, bf16[3,1024,256]{2,1,0:T(8,128)(2,1)S(1)}, u32[]{:S(2)}, u32[]{:S(2)}) collective-permute-start(bf16[3,1024,256]{2,1,0:T(8,128)(2,1)} %get-tuple-element.53.refs_16_), channel_id=1, source_target_pairs={{192,0},{0,64},{64,128},{128,192},{193,1},{1,65},{65,129},{129,193... | collective-permute-start | bytes 4718600 | tf_op jit(solution)/shard_map/ppermute | solution.py:21
  52.8 44.0 %collective-permute-start.9 = (bf16[3,1024,256]{2,1,0:T(8,128)(2,1)}, bf16[3,1024,256]{2,1,0:T(8,128)(2,1)}, u32[]{:S(2)}, u32[]{:S(2)}) collective-permute-start(bf16[3,1024,256]{2,1,0:T(8,128)(2,1)} %get-tuple-element.53.refs_16_), channel_id=1, source_target_pairs={{64,0},{128,64},{192,128},{0,192},{65,1},{129,65},{193,129},{1,193... | collective-permute-start | bytes 4718600 | tf_op jit(solution)/shard_map/ppermute | solution.py:21
  55.5 41.4 %collective-permute-start.11 = (bf16[1,4,64,1024]{3,2,1,0:T(8,128)(2,1)}, bf16[1,4,64,1024]{3,2,1,0:T(8,128)(2,1)}, u32[]{:S(2)}, u32[]{:S(2)}) collective-permute-start(bf16[1,4,64,1024]{3,2,1,0:T(8,128)(2,1)} %broadcast_select_fusion.1), channel_id=1, source_target_pairs={{2,0},{7,1},{4,2},{1,3},{6,4},{3,5},{0,6},{5,7},{10,8},{15,9},{12,... | collective-permute-start | bytes 1572872 | tf_op jit(solution)/shard_map/ppermute | solution.py:31
  58.5 38.4 %collective-permute-start.8 = (bf16[1,1024,256]{2,1,0:T(8,128)(2,1)}, bf16[1,1024,256]{2,1,0:T(8,128)(2,1)}, u32[]{:S(2)}, u32[]{:S(2)}) collective-permute-start(bf16[1,1024,256]{2,1,0:T(8,128)(2,1)} %get-tuple-element.54), channel_id=1, source_target_pairs={{16,0},{49,1},{32,16},{1,17},{48,32},{17,33},{0,48},{33,49},{18,2}... | collective-permute-start | bytes 1572872 | tf_op jit(solution)/shard_map/ppermute | solution.py:31
  62.7 62.1 %copy-start.4 = (f32[1,2048]{1,0:T(1,128)S(1)}, f32[1,2048]{1,0:T(1,128)}, u32[]{:S(2)}) copy-start(f32[1,2048]{1,0:T(1,128)} %p_ref.1) | copy-start | bytes 24580
  96.8 35.2 %copy-start.7 = (bf16[3,1024,256]{2,1,0:T(8,128)(2,1)}, bf16[3,1024,256]{2,1,0:T(8,128)(2,1)S(1)}, u32[]{:S(2)}) copy-start(bf16[3,1024,256]{2,1,0:T(8,128)(2,1)S(1)} %collective-permute-done.10.refs_19_) | copy-start | bytes 4718596
  104.9 75.8 %all-to-all-start = ((bf16[16,64,2048]{2,1,0:T(8,128)(2,1)}), bf16[16,64,2048]{2,1,0:T(8,128)(2,1)}, u32[]{:S(2)}, u32[]{:S(2)}) async-start(bf16[16,64,2048]{2,1,0:T(8,128)(2,1)} %split_points.2), calls=%async_computation | async-start | bytes 8388608 | tf_op jit(solution)/shard_map/all_to_all | solution.py:264
  124.5 11.1 %collective-permute-start.12 = (bf16[1,4,64,1024]{3,2,1,0:T(8,128)(2,1)}, bf16[1,4,64,1024]{3,2,1,0:T(8,128)(2,1)S(1)}, u32[]{:S(2)}, u32[]{:S(2)}) collective-permute-start(bf16[1,4,64,1024]{3,2,1,0:T(8,128)(2,1)} %refs_0_.1), channel_id=1, source_target_pairs={{0,1},{1,0},{2,3},{3,2},{4,5},{5,4},{6,7},{7,6},{8,9},{9,8},{10,11... | collective-permute-start | bytes 1572872 | tf_op jit(solution)/shard_map/ppermute | solution.py:16
  130.0 14.5 %collective-permute-start.21 = (bf16[1,1024,256]{2,1,0:T(8,128)(2,1)}, bf16[1,1024,256]{2,1,0:T(8,128)(2,1)S(1)}, u32[]{:S(2)}, u32[]{:S(2)}) collective-permute-start(bf16[1,1024,256]{2,1,0:T(8,128)(2,1)} %collective-permute-done.8.refs_20_), channel_id=1, source_target_pairs={{64,0},{128,64},{192,128},{0,192},{65,1},{129,65},{193,129},{1,193... | collective-permute-start | bytes 1572872 | tf_op jit(solution)/shard_map/ppermute | solution.py:21
  130.5 15.0 %collective-permute-start.22 = (bf16[1,1024,256]{2,1,0:T(8,128)(2,1)}, bf16[1,1024,256]{2,1,0:T(8,128)(2,1)S(1)}, u32[]{:S(2)}, u32[]{:S(2)}) collective-permute-start(bf16[1,1024,256]{2,1,0:T(8,128)(2,1)} %collective-permute-done.8.refs_20_), channel_id=1, source_target_pairs={{192,0},{0,64},{64,128},{128,192},{193,1},{1,65},{65,129},{129,193... | collective-permute-start | bytes 1572872 | tf_op jit(solution)/shard_map/ppermute | solution.py:21
  134.9 32.2 %collective-permute-start.20 = (bf16[3,1024,256]{2,1,0:T(8,128)(2,1)}, bf16[3,1024,256]{2,1,0:T(8,128)(2,1)S(1)}, u32[]{:S(2)}, u32[]{:S(2)}) collective-permute-start(bf16[3,1024,256]{2,1,0:T(8,128)(2,1)} %broadcast_select_fusion), channel_id=1, source_target_pairs={{64,0},{193,1},{128,64},{1,65},{192,128},{65,129},{0,192},{129,193... | collective-permute-start | bytes 4718600 | tf_op jit(solution)/shard_map/ppermute | solution.py:31
  135.4 11.1 %collective-permute-start.13 = (bf16[1,4,64,1024]{3,2,1,0:T(8,128)(2,1)S(1)}, bf16[1,4,64,1024]{3,2,1,0:T(8,128)(2,1)S(1)}, u32[]{:S(2)}, u32[]{:S(2)}) collective-permute-start(bf16[1,4,64,1024]{3,2,1,0:T(8,128)(2,1)S(1)} %copy-done.14), channel_id=1, source_target_pairs={{0,1},{1,0},{2,3},{3,2},{4,5},{5,4},{6,7},{7,6},{8,9},{9,8},{10,11... | collective-permute-start | bytes 1572872 | tf_op jit(solution)/shard_map/ppermute | solution.py:16
  135.6 11.3 %collective-permute-start.14 = (bf16[1,4,64,1024]{3,2,1,0:T(8,128)(2,1)S(1)}, bf16[1,4,64,1024]{3,2,1,0:T(8,128)(2,1)S(1)}, u32[]{:S(2)}, u32[]{:S(2)}) collective-permute-start(bf16[1,4,64,1024]{3,2,1,0:T(8,128)(2,1)S(1)} %collective-permute-done.5.refs_2_), channel_id=1, source_target_pairs={{0,1},{1,0},{2,3},{3,2},{4,5},{5,4},{6,7},{7,6},{8,9},{9,8},{10,11... | collective-permute-start | bytes 1572872 | tf_op jit(solution)/shard_map/ppermute | solution.py:16
  144.5 2.4 %collective-permute-start.16 = (bf16[1,4,64,1024]{3,2,1,0:T(8,128)(2,1)S(1)}, bf16[1,4,64,1024]{3,2,1,0:T(8,128)(2,1)S(1)}, u32[]{:S(2)}, u32[]{:S(2)}) collective-permute-start(bf16[1,4,64,1024]{3,2,1,0:T(8,128)(2,1)S(1)} %collective-permute-done.6.refs_4_), channel_id=1, source_target_pairs={{0,1},{1,0},{2,3},{3,2},{4,5},{5,4},{6,7},{7,6},{8,9},{9,8},{10,11... | collective-permute-start | bytes 1572872 | tf_op jit(solution)/shard_map/ppermute | solution.py:16
  145.5 2.1 collective-permute-start.15
  146.4 4.3 %collective-permute-start.17 = (bf16[1,4,64,1024]{3,2,1,0:T(8,128)(2,1)}, bf16[1,4,64,1024]{3,2,1,0:T(8,128)(2,1)}, u32[]{:S(2)}, u32[]{:S(2)}) collective-permute-start(bf16[1,4,64,1024]{3,2,1,0:T(8,128)(2,1)} %collective-permute-done.4.refs_5_), channel_id=1, source_target_pairs={{0,1},{1,0},{2,3},{3,2},{4,5},{5,4},{6,7},{7,6},{8,9},{9,8},{10,11... | collective-permute-start | bytes 1572872 | tf_op jit(solution)/shard_map/ppermute | solution.py:16
  146.9 3.9 %collective-permute-start.18 = (bf16[1,4,64,1024]{3,2,1,0:T(8,128)(2,1)}, bf16[1,4,64,1024]{3,2,1,0:T(8,128)(2,1)S(1)}, u32[]{:S(2)}, u32[]{:S(2)}) collective-permute-start(bf16[1,4,64,1024]{3,2,1,0:T(8,128)(2,1)} %collective-permute-done.7.refs_6_), channel_id=1, source_target_pairs={{0,1},{1,0},{2,3},{3,2},{4,5},{5,4},{6,7},{7,6},{8,9},{9,8},{10,11... | collective-permute-start | bytes 1572872 | tf_op jit(solution)/shard_map/ppermute | solution.py:16
  147.0 3.8 %collective-permute-start.19 = (bf16[1,4,64,1024]{3,2,1,0:T(8,128)(2,1)}, bf16[1,4,64,1024]{3,2,1,0:T(8,128)(2,1)}, u32[]{:S(2)}, u32[]{:S(2)}) collective-permute-start(bf16[1,4,64,1024]{3,2,1,0:T(8,128)(2,1)} %collective-permute-done.11.refs_7_), channel_id=1, source_target_pairs={{0,1},{1,0},{2,3},{3,2},{4,5},{5,4},{6,7},{7,6},{8,9},{9,8},{10,11... | collective-permute-start | bytes 1572872 | tf_op jit(solution)/shard_map/ppermute | solution.py:16
  148.6 18.5 %collective-permute-start.23 = (bf16[1,1024,256]{2,1,0:T(8,128)(2,1)}, bf16[1,1024,256]{2,1,0:T(8,128)(2,1)}, u32[]{:S(2)}, u32[]{:S(2)}) collective-permute-start(bf16[1,1024,256]{2,1,0:T(8,128)(2,1)} %broadcast_select_fusion.3), channel_id=1, source_target_pairs={{64,0},{193,1},{128,64},{1,65},{192,128},{65,129},{0,192},{129,193... | collective-permute-start | bytes 1572872 | tf_op jit(solution)/shard_map/ppermute | solution.py:31
  187.6 3.1 %collective-permute-start.24 = (f32[8,10,16,256]{3,2,1,0:T(8,128)S(1)}, f32[8,10,16,256]{3,2,1,0:T(8,128)S(1)}, u32[]{:S(2)}, u32[]{:S(2)}) collective-permute-start(f32[8,10,16,256]{3,2,1,0:T(8,128)S(1)} %get-tuple-element.51), channel_id=1, source_target_pairs={{0,1},{1,0},{2,3},{3,2},{4,5},{5,4},{6,7},{7,6},{8,9},{9,8},{10,11... | collective-permute-start | bytes 3932168 | tf_op jit(solution)/shard_map/ppermute | solution.py:16
  227.5 2.1 collective-permute-start.25
  (18 other events, 146.7 us)
